TPU v7x, 32 devices: a whole 2x2x4 slice. The times are simulated.
32 devices in a mesh: src: 4 (over y, x), tgt: 8 (over z, core).
Axes of the slice: x: 2, y: 2, z: 4, core: 2. Of those that a mesh axis runs over, the one named last changes fastest.
Arguments:
- pcs_source: bfloat16 [30, 8192], P(None, 'src'), may hold values from -6 to 10
- pcs_target: bfloat16 [30, 16384], P(None, 'tgt'), may hold values from -6 to 6
- growth: float32 [8192], P('src'), may hold values from 0.25 to 4
- scores: bfloat16 [8192, 128], P('src'), may hold values from -6 to 6
Outputs:
- source_potential: float32 [8192], P('src')
- target_potential: float32 [16384], P('tgt')
- transported: float32 [16384, 128], P('tgt')
All inputs are finite; a program needn't handle non-finite values.
Results may differ from a plain program's by a relative error of at most 0.0029.
Values sent between devices are 32-bit elements; how exact they have to be, the bound alone decides.
A program may use at most 64 MiB of HBM per device.

v0:
```python
import functools
import math

import jax
import jax.numpy as jnp
from jax import lax
from jax.experimental import pallas as pl
from jax.experimental.pallas import tpu as pltpu
from jax.sharding import PartitionSpec as P

ITERS = 2
EPSILON = 0.05
MARGIN = 1.0
FACTOR = MARGIN / (MARGIN + EPSILON)
LANES = 128
LOG2E = math.log2(math.e)
UNIT = EPSILON / LOG2E
MESH = pl.DeviceIdType.MESH
WIDTH, STEP, SUB = 512, 256, 64
DEPTH = 2048


def augment(coords_ref, wide_ref, rows_ref, columns_ref, norm_first):
    pcs, cells = coords_ref.shape
    wide = coords_ref[...].astype(jnp.float32)
    norm = -0.5 * jnp.sum(wide * wide, axis=0, keepdims=True)
    high = norm.astype(jnp.bfloat16).astype(jnp.float32)
    mid = (norm - high).astype(jnp.bfloat16).astype(jnp.float32)
    low = norm - high - mid
    base = -(-pcs // 8) * 8
    at = lax.broadcasted_iota(jnp.int32, (8, cells), 0) - (0 if norm_first else 3)
    one = jnp.where((at >= 3) & (at < 6) if norm_first else (at < 0), 1.0, 0.0)
    extra = jnp.where(at == 0, high, jnp.where(at == 1, mid, jnp.where(at == 2, low, one)))
    wide_ref[...] = jnp.zeros(wide_ref.shape, jnp.float32)
    wide_ref[0:pcs, :] = wide
    wide_ref[base : base + 8, :] = extra
    for k in range(cells // LANES):
        cut = slice(k * LANES, (k + 1) * LANES)
        piece = wide_ref[:, cut]
        rows_ref[cut, :] = piece.T.astype(jnp.bfloat16)
        columns_ref[:, cut] = piece.astype(jnp.bfloat16)


def spread(dense, out_ref):
    for k in range(dense.shape[0]):
        out_ref[k * LANES : (k + 1) * LANES, :] = jnp.broadcast_to(
            dense[k : k + 1, :], (LANES, LANES)
        ).T


def join(peak, total, block):
    t = block.reshape(-1, 8, LANES)
    newpeak = jnp.maximum(peak, jnp.max(t, axis=0))
    total = total * jnp.exp2(peak - newpeak) + jnp.sum(jnp.exp2(t - newpeak[None]), axis=0)
    return newpeak, total


def closed(peak, total):
    top = jnp.max(peak, axis=0, keepdims=True)
    return top, jnp.sum(total * jnp.exp2(peak - top), axis=0, keepdims=True)


def column_pass(tile_ref, bias_ref, lse_ref, make=None):
    rows, columns = tile_ref.shape
    width = math.gcd(columns, WIDTH)
    step = math.gcd(rows, STEP)
    sub = math.gcd(step, SUB)
    halves = width // LANES

    def over_columns(c, unused):
        start = pl.multiple_of(c * width, width)
        lanes = [pl.ds(pl.multiple_of(start + h * LANES, LANES), LANES) for h in range(halves)]

        def fill(r):
            at = pl.ds(r * step, step)
            tile_ref[at, pl.ds(start, width)] = make(at, pl.ds(start, width))

        empty = (jnp.full((8, LANES), -jnp.inf, jnp.float32), jnp.zeros((8, LANES), jnp.float32))
        stats = [empty] * halves
        if make is not None:
            fill(0)
        for r in range(rows // step):
            if make is not None and r + 1 < rows // step:
                fill(r + 1)
            for q in range(step // sub):
                at = pl.ds(r * step + q * sub, sub)
                for h in range(halves):
                    block = tile_ref[at, lanes[h]]
                    if bias_ref is not None:
                        block = block + bias_ref[at, :]
                    stats[h] = join(*stats[h], block)
        for h in range(halves):
            top, total = closed(*stats[h])
            lse_ref[pl.ds(c * halves + h, 1), :] = top + jnp.log2(total)
        return unused

    lax.fori_loop(0, columns // width, over_columns, 0)


def carry_tile(tile_ref, bias_ref, scores_ref, weights, start, width):
    rows = tile_ref.shape[0]
    halves = width // LANES
    sub = math.gcd(rows, SUB)
    step = math.gcd(rows, DEPTH)
    lanes = [pl.ds(pl.multiple_of(start + h * LANES, LANES), LANES) for h in range(halves)]
    peaks = [jnp.full((8, LANES), -jnp.inf, jnp.float32)] * halves
    for r in range(rows // sub):
        at = pl.ds(r * sub, sub)
        for h in range(halves):
            block = tile_ref[at, lanes[h]] + bias_ref[at, :]
            peaks[h] = jnp.maximum(peaks[h], jnp.max(block.reshape(-1, 8, LANES), axis=0))
    peaks = [jnp.max(peak, axis=0, keepdims=True) for peak in peaks]
    totals = [jnp.zeros((8, LANES), jnp.float32)] * halves
    for r in range(rows // sub):
        at = pl.ds(r * sub, sub)
        for h in range(halves):
            w = jnp.exp2(tile_ref[at, lanes[h]] + bias_ref[at, :] - peaks[h])
            totals[h] = totals[h] + jnp.sum(w.reshape(-1, 8, LANES), axis=0)
            weights[at, h * LANES : (h + 1) * LANES] = w.astype(jnp.bfloat16)
    carried = None
    for r in range(rows // step):
        at = slice(r * step, (r + 1) * step)
        part = jnp.dot(scores_ref[:, at], weights[at, 0:width], preferred_element_type=jnp.float32)
        carried = part if carried is None else carried + part
    return peaks, [jnp.sum(total, axis=0, keepdims=True) for total in totals], carried


def kernel(
    n_src, n_tgt, xs_ref, yt_ref, growth_ref, scores_ref, f_ref, g_ref, out_ref,
    tile, tile_t, wide, x_rows, x_cols, y_rows, y_cols, scores_t, bias, weights, partial,
    row_buf, col_buf, stat, received, row_send, row_recv, col_send, col_recv,
    stat_send, stat_recv, part_send, part_recv, out_send, out_recv,
):
    src, tgt = lax.axis_index("src"), lax.axis_index("tgt")
    barrier = pltpu.get_barrier_semaphore()
    for k in range(1, n_src):
        pl.semaphore_signal(
            barrier, inc=1, device_id={"src": lax.rem(src + k, n_src)}, device_id_type=MESH
        )
    for k in range(1, n_tgt):
        pl.semaphore_signal(
            barrier, inc=1, device_id={"tgt": lax.rem(tgt + k, n_tgt)}, device_id_type=MESH
        )

    rows, columns = tile.shape
    scale = 2.0 * LOG2E / (xs_ref.shape[0] * EPSILON)
    augment(xs_ref, wide.at[:, 0:rows], x_rows, x_cols, False)
    augment(yt_ref, wide.at[:, 0:columns], y_rows, y_cols, True)

    def filled(left, right):
        def make(at, lanes):
            return scale * lax.dot_general(
                left[at, :], right[:, lanes], (((1,), (0,)), ((), ())),
                preferred_element_type=jnp.float32,
            )
        return make

    def exchange(buf, axis, me, n, send, recv):
        copies = [
            pltpu.make_async_remote_copy(
                src_ref=buf.at[me], dst_ref=buf.at[me], send_sem=send.at[k], recv_sem=recv.at[k],
                device_id={axis: lax.rem(me + k, n)}, device_id_type=MESH,
            )
            for k in range(1, n)
        ]
        for copy in copies:
            copy.start()
        return copies

    def joined(buf, n):
        parts = [buf[d] for d in range(n)]
        top = functools.reduce(jnp.maximum, parts)
        return top + jnp.log2(sum(jnp.exp2(part - top) for part in parts))

    log_a = jnp.log2(growth_ref[...]) - math.log2(rows * n_src)
    log_b = -math.log2(columns * n_tgt)
    for step in range(ITERS):
        first = step == 0
        column_pass(
            tile_t, None if first else bias.at[0:columns, :], row_buf.at[step, tgt],
            filled(y_rows, x_cols) if first else None,
        )
        if first:
            pl.semaphore_wait(barrier, n_src + n_tgt - 2)
        copies = exchange(row_buf.at[step], "tgt", tgt, n_tgt, row_send.at[step], row_recv.at[step])
        if first:
            for k in range(rows // LANES):
                cut = slice(k * LANES, (k + 1) * LANES)
                scores_t[:, cut] = scores_ref[cut, :].astype(jnp.float32).T.astype(jnp.bfloat16)
        for copy in copies:
            copy.wait()
        potential = FACTOR * (log_a - joined(row_buf.at[step], n_tgt))
        spread(potential, bias)
        if step < ITERS - 1:
            column_pass(
                tile, bias.at[0:rows, :], col_buf.at[step, src],
                filled(x_rows, y_cols) if first else None,
            )
            copies = exchange(
                col_buf.at[step], "src", src, n_src, col_send.at[step], col_recv.at[step]
            )
            for copy in copies:
                copy.wait()
            spread(FACTOR * (log_b - joined(col_buf.at[step], n_src)), bias)
    f_ref[...] = UNIT * potential

    piece = columns // n_src
    width = math.gcd(piece, WIDTH)
    halves = width // LANES
    parts = []
    for k in range(1, n_src + 1):
        owner = lax.rem(src + k, n_src)

        def over_tiles(c, unused, owner=owner):
            start = pl.multiple_of(owner * piece + c * width, width)
            peaks, totals, carried = carry_tile(tile, bias, scores_t, weights, start, width)
            for h in range(halves):
                stat[src, 0, pl.ds(start // LANES + h, 1), :] = totals[h]
                stat[src, 1, pl.ds(start // LANES + h, 1), :] = peaks[h]
                at = pl.ds(pl.multiple_of(start + h * LANES, LANES), LANES)
                partial[at, :] = carried[:, h * LANES : (h + 1) * LANES].T
            return unused

        lax.fori_loop(0, piece // width, over_tiles, 0)
        if k < n_src:
            copy = pltpu.make_async_remote_copy(
                src_ref=partial.at[pl.ds(pl.multiple_of(owner * piece, piece), piece), :],
                dst_ref=received.at[k], send_sem=part_send.at[k], recv_sem=part_recv.at[k],
                device_id={"src": owner}, device_id_type=MESH,
            )
            copy.start()
            parts.append(copy)
    copies = exchange(stat, "src", src, n_src, stat_send, stat_recv)
    for copy in copies:
        copy.wait()
    peak = functools.reduce(jnp.maximum, [stat[d, 1] for d in range(n_src)])
    total = sum(stat[d, 0] * jnp.exp2(stat[d, 1] - peak) for d in range(n_src))
    g_ref[...] = UNIT * FACTOR * (log_b - (peak + jnp.log2(total)))
    for d in range(n_src):
        stat[d, 0] = jnp.exp2(stat[d, 1] - peak) / total
    for copy in parts:
        copy.wait()
    first_row = src * (piece // LANES)
    for q in range(piece // LANES):
        mine = pl.ds(pl.multiple_of(src * piece + q * LANES, LANES), LANES)
        result = None
        for k in range(n_src):
            sender = lax.rem(src - k + n_src, n_src)
            share = jnp.broadcast_to(
                stat[sender, 0, pl.ds(first_row + q, 1), :], (LANES, LANES)
            ).T
            block = partial[mine, :] if k == 0 else received[k, q * LANES : (q + 1) * LANES, :]
            result = share * block if result is None else result + share * block
        out_ref[mine, :] = result
    mine = pl.ds(pl.multiple_of(src * piece, piece), piece)
    copies = [
        pltpu.make_async_remote_copy(
            src_ref=out_ref.at[mine, :], dst_ref=out_ref.at[mine, :],
            send_sem=out_send.at[k], recv_sem=out_recv.at[k],
            device_id={"src": lax.rem(src + k, n_src)}, device_id_type=MESH,
        )
        for k in range(1, n_src)
    ]
    for copy in copies:
        copy.start()
    for copy in copies:
        copy.wait()


def solution(mesh):
    n_src, n_tgt = mesh.shape["src"], mesh.shape["tgt"]

    def shards(pcs_source, pcs_target, growth, scores):
        rows, columns = pcs_source.shape[1], pcs_target.shape[1]
        programs = scores.shape[1]
        piece = columns // n_src
        f32, bf16 = jnp.float32, jnp.bfloat16
        sem = pltpu.SemaphoreType.DMA
        whole = pl.BlockSpec(memory_space=pltpu.VMEM)
        dense_r, dense_c = (rows // LANES, LANES), (columns // LANES, LANES)
        f, g, out = pl.pallas_call(
            functools.partial(kernel, n_src, n_tgt),
            out_shape=(
                jax.ShapeDtypeStruct(dense_r, f32),
                jax.ShapeDtypeStruct(dense_c, f32),
                jax.ShapeDtypeStruct((columns, programs), f32),
            ),
            in_specs=[whole] * 4,
            out_specs=(whole,) * 3,
            scratch_shapes=[
                pltpu.VMEM((rows, columns), f32),
                pltpu.VMEM((columns, rows), f32),
                pltpu.VMEM((LANES, max(rows, columns)), f32),
                pltpu.VMEM((rows, LANES), bf16),
                pltpu.VMEM((LANES, rows), bf16),
                pltpu.VMEM((columns, LANES), bf16),
                pltpu.VMEM((LANES, columns), bf16),
                pltpu.VMEM((programs, rows), bf16),
                pltpu.VMEM((max(rows, columns), LANES), f32),
                pltpu.VMEM((rows, math.gcd(piece, WIDTH)), bf16),
                pltpu.VMEM((columns, programs), f32),
                pltpu.VMEM((ITERS, n_tgt) + dense_r, f32),
                pltpu.VMEM((ITERS, n_src) + dense_c, f32),
                pltpu.VMEM((n_src, 2) + dense_c, f32),
                pltpu.VMEM((n_src, piece, programs), f32),
                sem((ITERS, n_tgt)),
                sem((ITERS, n_tgt)),
                sem((ITERS, n_src)),
                sem((ITERS, n_src)),
                sem((n_src,)),
                sem((n_src,)),
                sem((n_src,)),
                sem((n_src,)),
                sem((n_src,)),
                sem((n_src,)),
            ],
            compiler_params=pltpu.CompilerParams(
                collective_id=0, has_side_effects=True, vmem_limit_bytes=60 * 2**20
            ),
            name="coupling",
        )(pcs_source, pcs_target, growth.reshape(dense_r), scores)
        return f.reshape(-1), g.reshape(-1), out

    in_specs = (P(None, "src"), P(None, "tgt"), P("src"), P("src", None))
    out_specs = (P("src"), P("tgt"), P("tgt", None))
    return jax.shard_map(shards, mesh=mesh, in_specs=in_specs, out_specs=out_specs, check_vma=False)
```

profile of v0, /device:TPU:0, one launch (start us, length us, event | category | flops | bytes accessed | tf_op | source)
XLA Modules:
  0.0 68.3 jit_solution(8162551155680361208)
XLA Ops:
  0.6 63.4 %coupling.1 = (f32[16,128]{1,0:T(8,128)}, f32[16,128]{1,0:T(8,128)}, f32[2048,128]{1,0:T(8,128)}) custom-call(bf16[30,2048]{1,0:T(8,128)(2,1)} %xs_ref.1, bf16[30,2048]{1,0:T(8,128)(2,1)} %yt_ref.1, f32[16,128]{1,0:T(8,128)} %bitcast.3, bf16[2048,128]{1,0:T(8,128)(2,1)} %scores_ref.1), custom_call_target="tpu_custom_call" | custom-call | tf_op jit(solution)/shard_map/coupling/pallas_call | solution.py:281
  64.0 0.0 copy-start.1
  64.0 0.7 %copy-done.1 = f32[16,128]{1,0:T(8,128)S(1)} copy-done((f32[16,128]{1,0:T(8,128)S(1)}, f32[16,128]{1,0:T(8,128)}, u32[]{:S(2)}) %copy-start.1) | copy-done | bytes 8216
  64.7 0.0 copy-start
  64.7 0.6 copy.10
  65.3 0.1 copy-done
  65.4 0.6 copy.11
  66.0 2.3 %copy.12 = f32[2048,128]{1,0:T(8,128)} copy(f32[2048,128]{1,0:T(8,128)} %get-tuple-element.14) | data formatting | bytes 2097152
Async XLA Ops:
  64.0 0.7 %copy-start.1 = (f32[16,128]{1,0:T(8,128)S(1)}, f32[16,128]{1,0:T(8,128)}, u32[]{:S(2)}) copy-start(f32[16,128]{1,0:T(8,128)} %get-tuple-element.6) | copy-start | bytes 24580
  64.7 0.7 %copy-start = (f32[16,128]{1,0:T(8,128)S(1)}, f32[16,128]{1,0:T(8,128)}, u32[]{:S(2)}) copy-start(f32[16,128]{1,0:T(8,128)} %get-tuple-element.7) | copy-start | bytes 24580
where the time goes:
time: 68.5 us; the launch traced here: 68.3 us
  Pallas kernels  63.4 us (93%)
  local copies, waits for them, and re-layouts  4.25 us (6%)
    pallas_call x1, Pallas kernels, shards(): pl.pallas_call(functools.partial(kernel, n_src, n_tgt), out_shape=(jax.Sh...  63.4 us
    unnamed x7, local copies, waits for them, and re-layouts  4.25 us

commit v1 on v0

v1 whole, which is shorter than its diff:
```python
import functools
import math

import jax
import jax.numpy as jnp
from jax import lax
from jax.experimental import pallas as pl
from jax.experimental.pallas import tpu as pltpu
from jax.sharding import PartitionSpec as P

ITERS = 2
EPSILON = 0.05
MARGIN = 1.0
FACTOR = MARGIN / (MARGIN + EPSILON)
LANES = 128
LOG2E = math.log2(math.e)
UNIT = EPSILON / LOG2E
MESH = pl.DeviceIdType.MESH
WIDTH, STEP, SUB = 512, 256, 64


def split3(value):
    high = value.astype(jnp.bfloat16).astype(jnp.float32)
    mid = (value - high).astype(jnp.bfloat16).astype(jnp.float32)
    return high, mid, value - high - mid


def depth_of(pcs):
    base = -(-pcs // 8) * 8
    return base, -(-(3 * base + 16) // LANES) * LANES


def augment(coords_ref, wide_ref, columns_ref, scale, source):
    pcs, cells = coords_ref.shape
    base, depth = depth_of(pcs)
    wide = coords_ref[...].astype(jnp.float32)
    norm = -0.5 * scale * jnp.sum(wide * wide, axis=0, keepdims=True)
    at = lax.broadcasted_iota(jnp.int32, (16, cells), 0) - (0 if source else 3)
    high, mid, low = split3(norm)
    extra = jnp.where(at == 0, high, jnp.where(at == 1, mid, jnp.where(at == 2, low, 0.0)))
    at = lax.broadcasted_iota(jnp.int32, (16, cells), 0)
    ones = ((at >= 3) & (at < 6)) | ((at >= 11) & (at < 14)) if source else (at < 3) | ((at >= 8) & (at < 11))
    wide_ref[...] = jnp.zeros(wide_ref.shape, jnp.float32)
    for k, piece in enumerate(split3(scale * wide) if source else (wide,) * 3):
        wide_ref[k * base : k * base + pcs, :] = piece
    wide_ref[3 * base : 3 * base + 16, :] = jnp.where(ones, 1.0, extra)
    columns_ref[...] = wide_ref[...].astype(jnp.bfloat16)


def turn(wide_ref, rows_ref):
    depth, cells = wide_ref.shape
    for k in range(cells // LANES):
        cut = slice(k * LANES, (k + 1) * LANES)
        for d in range(depth // LANES):
            deep = slice(d * LANES, (d + 1) * LANES)
            rows_ref[cut, deep] = wide_ref[deep, cut].T.astype(jnp.bfloat16)


def set_bias(dense, wide_ref, rows_ref, at):
    for p, piece in enumerate(split3(dense)):
        for k in range(dense.shape[0]):
            wide_ref[at + p : at + p + 1, k * LANES : (k + 1) * LANES] = piece[k : k + 1, :]
    turn(wide_ref, rows_ref)


def join(peak, total, block):
    t = block.reshape(-1, 8, LANES)
    newpeak = jnp.maximum(peak, jnp.max(t, axis=0))
    total = total * jnp.exp2(peak - newpeak) + jnp.sum(jnp.exp2(t - newpeak[None]), axis=0)
    return newpeak, total


def closed(peak, total):
    top = jnp.max(peak, axis=0, keepdims=True)
    return top, jnp.sum(total * jnp.exp2(peak - top), axis=0, keepdims=True)


def lse_pass(rows_ref, columns_ref, lse_ref):
    rows, columns = rows_ref.shape[0], columns_ref.shape[1]
    width = math.gcd(columns, WIDTH)
    step = math.gcd(rows, STEP)
    sub = math.gcd(step, SUB)
    halves = width // LANES

    def over_columns(c, unused):
        right = columns_ref[:, pl.ds(pl.multiple_of(c * width, width), width)]
        empty = (jnp.full((8, LANES), -jnp.inf, jnp.float32), jnp.zeros((8, LANES), jnp.float32))
        stats = [empty] * halves
        for r in range(rows // step):
            block = jnp.dot(
                rows_ref[r * step : (r + 1) * step, :], right, preferred_element_type=jnp.float32
            )
            for q in range(step // sub):
                for h in range(halves):
                    cut = block[q * sub : (q + 1) * sub, h * LANES : (h + 1) * LANES]
                    stats[h] = join(*stats[h], cut)
        for h in range(halves):
            top, total = closed(*stats[h])
            lse_ref[pl.ds(c * halves + h, 1), :] = top + jnp.log2(total)
        return unused

    lax.fori_loop(0, columns // width, over_columns, 0)


def fill_tile(rows_ref, right, tile_ref):
    rows, width = tile_ref.shape
    step = math.gcd(rows, STEP)
    peak = jnp.full((8, width), -jnp.inf, jnp.float32)
    for r in range(rows // step):
        at = slice(r * step, (r + 1) * step)
        block = jnp.dot(rows_ref[at, :], right, preferred_element_type=jnp.float32)
        tile_ref[at, :] = block
        peak = jnp.maximum(peak, jnp.max(block.reshape(-1, 8, width), axis=0))
    return jnp.max(peak, axis=0, keepdims=True)


def carry_tile(tile_ref, peak, scores_ref, weights):
    rows = tile_ref.shape[0]
    step = math.gcd(rows, STEP)
    for r in range(rows // step):
        at = slice(r * step, (r + 1) * step)
        weights[at, :] = jnp.exp2(tile_ref[at, :] - peak).astype(jnp.bfloat16)
    return jnp.dot(scores_ref[...], weights[...], preferred_element_type=jnp.float32)


def kernel(
    n_src, n_tgt, xs_ref, yt_ref, growth_ref, scores_ref, f_ref, g_ref, out_ref,
    tile, x_wide, y_wide, x_rows, x_cols, y_rows, y_cols, scores_t, weights, partial,
    row_buf, col_buf, stat, received, row_send, row_recv, col_send, col_recv,
    stat_send, stat_recv, part_send, part_recv, out_send, out_recv,
):
    src, tgt = lax.axis_index("src"), lax.axis_index("tgt")
    barrier = pltpu.get_barrier_semaphore()
    for k in range(1, n_src):
        pl.semaphore_signal(
            barrier, inc=1, device_id={"src": lax.rem(src + k, n_src)}, device_id_type=MESH
        )
    for k in range(1, n_tgt):
        pl.semaphore_signal(
            barrier, inc=1, device_id={"tgt": lax.rem(tgt + k, n_tgt)}, device_id_type=MESH
        )

    pcs, rows = xs_ref.shape
    columns = yt_ref.shape[1]
    programs = scores_ref.shape[1]
    scale = 2.0 * LOG2E / (pcs * EPSILON)
    bias_at = 3 * depth_of(pcs)[0] + 8
    augment(yt_ref, y_wide, y_cols, scale, False)
    turn(y_wide, y_rows)
    augment(xs_ref, x_wide, x_cols, scale, True)

    def exchange(buf, axis, me, n, send, recv):
        copies = [
            pltpu.make_async_remote_copy(
                src_ref=buf.at[me], dst_ref=buf.at[me], send_sem=send.at[k], recv_sem=recv.at[k],
                device_id={axis: lax.rem(me + k, n)}, device_id_type=MESH,
            )
            for k in range(1, n)
        ]
        for copy in copies:
            copy.start()
        return copies

    def joined(buf, n):
        parts = [buf[d] for d in range(n)]
        top = functools.reduce(jnp.maximum, parts)
        return top + jnp.log2(sum(jnp.exp2(part - top) for part in parts))

    log_a = jnp.log2(growth_ref[...]) - math.log2(rows * n_src)
    log_b = -math.log2(columns * n_tgt)
    for step in range(ITERS):
        first = step == 0
        lse_pass(y_rows, x_cols, row_buf.at[step, tgt])
        if first:
            pl.semaphore_wait(barrier, n_src + n_tgt - 2)
        copies = exchange(row_buf.at[step], "tgt", tgt, n_tgt, row_send.at[step], row_recv.at[step])
        if first:
            for k in range(rows // LANES):
                cut = slice(k * LANES, (k + 1) * LANES)
                scores_t[0:programs, cut] = scores_ref[cut, :].astype(jnp.float32).T.astype(jnp.bfloat16)
            scores_t[programs:, :] = jnp.ones((16, rows), jnp.bfloat16)
        for copy in copies:
            copy.wait()
        potential = FACTOR * (log_a - joined(row_buf.at[step], n_tgt))
        set_bias(potential, x_wide, x_rows, bias_at)
        if step < ITERS - 1:
            lse_pass(x_rows, y_cols, col_buf.at[step, src])
            copies = exchange(
                col_buf.at[step], "src", src, n_src, col_send.at[step], col_recv.at[step]
            )
            for copy in copies:
                copy.wait()
            set_bias(FACTOR * (log_b - joined(col_buf.at[step], n_src)), y_wide, y_rows, bias_at + 3)
    f_ref[...] = UNIT * potential

    piece = columns // n_src
    width = math.gcd(piece, WIDTH)
    halves = width // LANES
    parts = []

    def fill(unit):
        k, c = divmod(unit, piece // width)
        start = lax.rem(src + k + 1, n_src) * piece + c * width
        start = pl.multiple_of(start, width)
        right = y_cols[:, pl.ds(start, width)]
        return start, fill_tile(x_rows, right, tile.at[unit % 2])

    units = n_src * (piece // width)
    ready = fill(0)
    for unit in range(units):
        start, peak = ready
        if unit + 1 < units:
            ready = fill(unit + 1)
        carried = carry_tile(tile.at[unit % 2], peak, scores_t, weights.at[unit % 2])
        for h in range(halves):
            lanes = slice(h * LANES, (h + 1) * LANES)
            stat[src, 0, pl.ds(start // LANES + h, 1), :] = carried[programs : programs + 1, lanes]
            stat[src, 1, pl.ds(start // LANES + h, 1), :] = peak[:, lanes]
            at = pl.ds(pl.multiple_of(start + h * LANES, LANES), LANES)
            partial[at, :] = carried[0:programs, lanes].T
        k = (unit + 1) * width // piece
        owner = lax.rem(src + k, n_src)
        if (unit + 1) * width % piece:
            continue
        if k < n_src:
            copy = pltpu.make_async_remote_copy(
                src_ref=partial.at[pl.ds(pl.multiple_of(owner * piece, piece), piece), :],
                dst_ref=received.at[k], send_sem=part_send.at[k], recv_sem=part_recv.at[k],
                device_id={"src": owner}, device_id_type=MESH,
            )
            copy.start()
            parts.append(copy)
    copies = exchange(stat, "src", src, n_src, stat_send, stat_recv)
    for copy in copies:
        copy.wait()
    peak = functools.reduce(jnp.maximum, [stat[d, 1] for d in range(n_src)])
    total = sum(stat[d, 0] * jnp.exp2(stat[d, 1] - peak) for d in range(n_src))
    g_ref[...] = UNIT * FACTOR * (log_b - (peak + jnp.log2(total)))
    for d in range(n_src):
        stat[d, 0] = jnp.exp2(stat[d, 1] - peak) / total
    for copy in parts:
        copy.wait()
    first_row = src * (piece // LANES)
    for q in range(piece // LANES):
        mine = pl.ds(pl.multiple_of(src * piece + q * LANES, LANES), LANES)
        result = None
        for k in range(n_src):
            sender = lax.rem(src - k + n_src, n_src)
            share = jnp.broadcast_to(
                stat[sender, 0, pl.ds(first_row + q, 1), :], (LANES, LANES)
            ).T
            block = partial[mine, :] if k == 0 else received[k, q * LANES : (q + 1) * LANES, :]
            result = share * block if result is None else result + share * block
        out_ref[mine, :] = result
    mine = pl.ds(pl.multiple_of(src * piece, piece), piece)
    copies = [
        pltpu.make_async_remote_copy(
            src_ref=out_ref.at[mine, :], dst_ref=out_ref.at[mine, :],
            send_sem=out_send.at[k], recv_sem=out_recv.at[k],
            device_id={"src": lax.rem(src + k, n_src)}, device_id_type=MESH,
        )
        for k in range(1, n_src)
    ]
    for copy in copies:
        copy.start()
    for copy in copies:
        copy.wait()


def solution(mesh):
    n_src, n_tgt = mesh.shape["src"], mesh.shape["tgt"]

    def shards(pcs_source, pcs_target, growth, scores):
        rows, columns = pcs_source.shape[1], pcs_target.shape[1]
        programs = scores.shape[1]
        piece = columns // n_src
        width = math.gcd(piece, WIDTH)
        depth = depth_of(pcs_source.shape[0])[1]
        f32, bf16 = jnp.float32, jnp.bfloat16
        sem = pltpu.SemaphoreType.DMA
        whole = pl.BlockSpec(memory_space=pltpu.VMEM)
        dense_r, dense_c = (rows // LANES, LANES), (columns // LANES, LANES)
        f, g, out = pl.pallas_call(
            functools.partial(kernel, n_src, n_tgt),
            out_shape=(
                jax.ShapeDtypeStruct(dense_r, f32),
                jax.ShapeDtypeStruct(dense_c, f32),
                jax.ShapeDtypeStruct((columns, programs), f32),
            ),
            in_specs=[whole] * 4,
            out_specs=(whole,) * 3,
            scratch_shapes=[
                pltpu.VMEM((2, rows, width), f32),
                pltpu.VMEM((depth, rows), f32),
                pltpu.VMEM((depth, columns), f32),
                pltpu.VMEM((rows, depth), bf16),
                pltpu.VMEM((depth, rows), bf16),
                pltpu.VMEM((columns, depth), bf16),
                pltpu.VMEM((depth, columns), bf16),
                pltpu.VMEM((programs + 16, rows), bf16),
                pltpu.VMEM((2, rows, width), bf16),
                pltpu.VMEM((columns, programs), f32),
                pltpu.VMEM((ITERS, n_tgt) + dense_r, f32),
                pltpu.VMEM((ITERS, n_src) + dense_c, f32),
                pltpu.VMEM((n_src, 2) + dense_c, f32),
                pltpu.VMEM((n_src, piece, programs), f32),
                sem((ITERS, n_tgt)),
                sem((ITERS, n_tgt)),
                sem((ITERS, n_src)),
                sem((ITERS, n_src)),
                sem((n_src,)),
                sem((n_src,)),
                sem((n_src,)),
                sem((n_src,)),
                sem((n_src,)),
                sem((n_src,)),
            ],
            compiler_params=pltpu.CompilerParams(
                collective_id=0, has_side_effects=True, vmem_limit_bytes=60 * 2**20
            ),
            name="coupling",
        )(pcs_source, pcs_target, growth.reshape(dense_r), scores)
        return f.reshape(-1), g.reshape(-1), out

    in_specs = (P(None, "src"), P(None, "tgt"), P("src"), P("src", None))
    out_specs = (P("src"), P("tgt"), P("tgt", None))
    return jax.shard_map(shards, mesh=mesh, in_specs=in_specs, out_specs=out_specs, check_vma=False)
```

time: 68.5 us -> 63.2 us (0.923)
  Pallas kernels: 63.4 us -> 58 us
    pallas_call x1, Pallas kernels: 63.4 us -> 58 us  [shards(): pl.pallas_call(functools.partial(kernel, n_src, n_tgt), out_shape=(jax.Sh...]
where the time goes in v1:
time: 63.2 us; the launch traced here: 62.9 us
  Pallas kernels  58 us (92%)
  local copies, waits for them, and re-layouts  4.25 us (7%)
  between operations  0.65 us (1%)
    pallas_call x1, Pallas kernels, shards(): pl.pallas_call(functools.partial(kernel, n_src, n_tgt), out_shape=(jax.Sh...  58 us
    unnamed x7, local copies, waits for them, and re-layouts  4.25 us

profile of v1, /device:TPU:0, one launch (start us, length us, event | category | flops | bytes accessed | tf_op | source)
XLA Modules:
  0.0 62.9 jit_solution(5751163102931137813)
XLA Ops:
  0.6 58.0 %coupling.1 = (f32[16,128]{1,0:T(8,128)}, f32[16,128]{1,0:T(8,128)}, f32[2048,128]{1,0:T(8,128)}) custom-call(bf16[30,2048]{1,0:T(8,128)(2,1)} %xs_ref.1, bf16[30,2048]{1,0:T(8,128)(2,1)} %yt_ref.1, f32[16,128]{1,0:T(8,128)} %bitcast.3, bf16[2048,128]{1,0:T(8,128)(2,1)} %scores_ref.1), custom_call_target="tpu_custom_call" | custom-call | tf_op jit(solution)/shard_map/coupling/pallas_call | solution.py:283
  58.7 0.0 copy-start.1
  58.7 0.7 %copy-done.1 = f32[16,128]{1,0:T(8,128)S(1)} copy-done((f32[16,128]{1,0:T(8,128)S(1)}, f32[16,128]{1,0:T(8,128)}, u32[]{:S(2)}) %copy-start.1) | copy-done | bytes 8216
  59.4 0.0 copy-start
  59.4 0.6 copy.10
  60.0 0.1 copy-done
  60.1 0.6 copy.11
  60.7 2.3 %copy.12 = f32[2048,128]{1,0:T(8,128)} copy(f32[2048,128]{1,0:T(8,128)} %get-tuple-element.14) | data formatting | bytes 2097152
Async XLA Ops:
  58.7 0.7 %copy-start.1 = (f32[16,128]{1,0:T(8,128)S(1)}, f32[16,128]{1,0:T(8,128)}, u32[]{:S(2)}) copy-start(f32[16,128]{1,0:T(8,128)} %get-tuple-element.6) | copy-start | bytes 24580
  59.4 0.7 %copy-start = (f32[16,128]{1,0:T(8,128)S(1)}, f32[16,128]{1,0:T(8,128)}, u32[]{:S(2)}) copy-start(f32[16,128]{1,0:T(8,128)} %get-tuple-element.7) | copy-start | bytes 24580

commit v2 on v1

--- a/solution.py
+++ b/solution.py
@@ -47,20 +47,27 @@
     columns_ref[...] = wide_ref[...].astype(jnp.bfloat16)
 
 
-def turn(wide_ref, rows_ref):
-    depth, cells = wide_ref.shape
-    for k in range(cells // LANES):
+def turn(wide_ref, rows_ref, first, last):
+    depth = wide_ref.shape[0]
+    for k in range(first // LANES, last // LANES):
         cut = slice(k * LANES, (k + 1) * LANES)
         for d in range(depth // LANES):
             deep = slice(d * LANES, (d + 1) * LANES)
             rows_ref[cut, deep] = wide_ref[deep, cut].T.astype(jnp.bfloat16)
 
 
-def set_bias(dense, wide_ref, rows_ref, at):
+def set_bias(dense, wide_ref, rows_ref, at, first):
+    cells = dense.shape[0] * LANES
     for p, piece in enumerate(split3(dense)):
         for k in range(dense.shape[0]):
-            wide_ref[at + p : at + p + 1, k * LANES : (k + 1) * LANES] = piece[k : k + 1, :]
-    turn(wide_ref, rows_ref)
+            lanes = slice(first + k * LANES, first + (k + 1) * LANES)
+            wide_ref[at + p : at + p + 1, lanes] = piece[k : k + 1, :]
+    turn(wide_ref, rows_ref, first, first + cells)
+
+
+def halves_of(cells):
+    parts = math.gcd(2, max(cells // (8 * LANES), 1))
+    return [(p * (cells // parts), (p + 1) * (cells // parts)) for p in range(parts)]
 
 
 def join(peak, total, block):
@@ -75,43 +82,52 @@
     return top, jnp.sum(total * jnp.exp2(peak - top), axis=0, keepdims=True)
 
 
-def lse_pass(rows_ref, columns_ref, lse_ref):
-    rows, columns = rows_ref.shape[0], columns_ref.shape[1]
-    width = math.gcd(columns, WIDTH)
-    step = math.gcd(rows, STEP)
+def lse_pass(rows_ref, columns_ref, stats_ref, lse_ref, row_span, lane_span, fresh):
+    (low, high), (begin, end) = row_span, lane_span
+    width = math.gcd(end - begin, WIDTH)
+    step = math.gcd(high - low, STEP)
     sub = math.gcd(step, SUB)
     halves = width // LANES
 
     def over_columns(c, unused):
-        right = columns_ref[:, pl.ds(pl.multiple_of(c * width, width), width)]
-        empty = (jnp.full((8, LANES), -jnp.inf, jnp.float32), jnp.zeros((8, LANES), jnp.float32))
-        stats = [empty] * halves
-        for r in range(rows // step):
+        right = columns_ref[:, pl.ds(pl.multiple_of(begin + c * width, width), width)]
+        tiles = [begin // LANES + c * halves + h for h in range(halves)]
+        if fresh:
+            empty = (jnp.full((8, LANES), -jnp.inf, jnp.float32), jnp.zeros((8, LANES), jnp.float32))
+            stats = [empty] * halves
+        else:
+            stats = [(stats_ref[0, tile], stats_ref[1, tile]) for tile in tiles]
+        for r in range((high - low) // step):
             block = jnp.dot(
-                rows_ref[r * step : (r + 1) * step, :], right, preferred_element_type=jnp.float32
+                rows_ref[low + r * step : low + (r + 1) * step, :], right,
+                preferred_element_type=jnp.float32,
             )
             for q in range(step // sub):
                 for h in range(halves):
                     cut = block[q * sub : (q + 1) * sub, h * LANES : (h + 1) * LANES]
                     stats[h] = join(*stats[h], cut)
-        for h in range(halves):
-            top, total = closed(*stats[h])
-            lse_ref[pl.ds(c * halves + h, 1), :] = top + jnp.log2(total)
+        for tile, (peak, total) in zip(tiles, stats):
+            if lse_ref is None:
+                stats_ref[0, tile] = peak
+                stats_ref[1, tile] = total
+            else:
+                top, total = closed(peak, total)
+                lse_ref[pl.ds(tile, 1), :] = top + jnp.log2(total)
         return unused
 
-    lax.fori_loop(0, columns // width, over_columns, 0)
-
-
-def fill_tile(rows_ref, right, tile_ref):
-    rows, width = tile_ref.shape
-    step = math.gcd(rows, STEP)
-    peak = jnp.full((8, width), -jnp.inf, jnp.float32)
-    for r in range(rows // step):
-        at = slice(r * step, (r + 1) * step)
+    lax.fori_loop(0, (end - begin) // width, over_columns, 0)
+
+
+def fill_tile(rows_ref, right, tile_ref, row_span, peak):
+    low, high = row_span
+    width = tile_ref.shape[1]
+    step = math.gcd(high - low, STEP)
+    for r in range((high - low) // step):
+        at = slice(low + r * step, low + (r + 1) * step)
         block = jnp.dot(rows_ref[at, :], right, preferred_element_type=jnp.float32)
         tile_ref[at, :] = block
         peak = jnp.maximum(peak, jnp.max(block.reshape(-1, 8, width), axis=0))
-    return jnp.max(peak, axis=0, keepdims=True)
+    return peak
 
 
 def carry_tile(tile_ref, peak, scores_ref, weights):
@@ -125,7 +141,7 @@
 
 def kernel(
     n_src, n_tgt, xs_ref, yt_ref, growth_ref, scores_ref, f_ref, g_ref, out_ref,
-    tile, x_wide, y_wide, x_rows, x_cols, y_rows, y_cols, scores_t, weights, partial,
+    tile, x_wide, y_wide, x_rows, x_cols, y_rows, y_cols, scores_t, weights, partial, running,
     row_buf, col_buf, stat, received, row_send, row_recv, col_send, col_recv,
     stat_send, stat_recv, part_send, part_recv, out_send, out_recv,
 ):
@@ -146,13 +162,14 @@
     scale = 2.0 * LOG2E / (pcs * EPSILON)
     bias_at = 3 * depth_of(pcs)[0] + 8
     augment(yt_ref, y_wide, y_cols, scale, False)
-    turn(y_wide, y_rows)
+    turn(y_wide, y_rows, 0, columns)
     augment(xs_ref, x_wide, x_cols, scale, True)
 
-    def exchange(buf, axis, me, n, send, recv):
+    def exchange(buf, axis, me, n, send, recv, lines):
         copies = [
             pltpu.make_async_remote_copy(
-                src_ref=buf.at[me], dst_ref=buf.at[me], send_sem=send.at[k], recv_sem=recv.at[k],
+                src_ref=buf.at[me, lines], dst_ref=buf.at[me, lines],
+                send_sem=send.at[k], recv_sem=recv.at[k],
                 device_id={axis: lax.rem(me + k, n)}, device_id_type=MESH,
             )
             for k in range(1, n)
@@ -161,56 +178,89 @@
             copy.start()
         return copies
 
-    def joined(buf, n):
-        parts = [buf[d] for d in range(n)]
+    def joined(buf, n, lines):
+        parts = [buf[d, lines] for d in range(n)]
         top = functools.reduce(jnp.maximum, parts)
         return top + jnp.log2(sum(jnp.exp2(part - top) for part in parts))
 
     log_a = jnp.log2(growth_ref[...]) - math.log2(rows * n_src)
     log_b = -math.log2(columns * n_tgt)
+    source_halves, target_halves = halves_of(rows), halves_of(columns)
+
+    def lines_of(span):
+        return slice(span[0] // LANES, span[1] // LANES)
+
+    def finish(rows_ref, columns_ref, row_span, spans, fresh, buf, axis, me, n, send, recv, enter=False):
+        sent = []
+        for h, span in enumerate(spans):
+            lse_pass(rows_ref, columns_ref, running, buf.at[me], row_span, span, fresh)
+            if enter and h == 0:
+                pl.semaphore_wait(barrier, n_src + n_tgt - 2)
+            sent.append(exchange(buf, axis, me, n, send.at[h], recv.at[h], lines_of(span)))
+        return sent
+
+    def settle(copies):
+        for copy in copies:
+            copy.wait()
+
     for step in range(ITERS):
-        first = step == 0
-        lse_pass(y_rows, x_cols, row_buf.at[step, tgt])
-        if first:
-            pl.semaphore_wait(barrier, n_src + n_tgt - 2)
-        copies = exchange(row_buf.at[step], "tgt", tgt, n_tgt, row_send.at[step], row_recv.at[step])
-        if first:
+        over_tgt = (row_buf.at[step], "tgt", tgt, n_tgt, row_send.at[step], row_recv.at[step])
+        over_src = (col_buf.at[step], "src", src, n_src, col_send.at[step], col_recv.at[step])
+        if step == 0:
+            sent = finish(
+                y_rows, x_cols, (0, columns), source_halves, True, *over_tgt, enter=True
+            )
             for k in range(rows // LANES):
                 cut = slice(k * LANES, (k + 1) * LANES)
                 scores_t[0:programs, cut] = scores_ref[cut, :].astype(jnp.float32).T.astype(jnp.bfloat16)
             scores_t[programs:, :] = jnp.ones((16, rows), jnp.bfloat16)
-        for copy in copies:
-            copy.wait()
-        potential = FACTOR * (log_a - joined(row_buf.at[step], n_tgt))
-        set_bias(potential, x_wide, x_rows, bias_at)
-        if step < ITERS - 1:
-            lse_pass(x_rows, y_cols, col_buf.at[step, src])
-            copies = exchange(
-                col_buf.at[step], "src", src, n_src, col_send.at[step], col_recv.at[step]
-            )
-            for copy in copies:
-                copy.wait()
-            set_bias(FACTOR * (log_b - joined(col_buf.at[step], n_src)), y_wide, y_rows, bias_at + 3)
-    f_ref[...] = UNIT * potential
+        else:
+            for h, span in enumerate(target_halves):
+                settle(sent[h])
+                lines = lines_of(span)
+                g = FACTOR * (log_b - joined(col_buf.at[step - 1], n_src, lines))
+                set_bias(g, y_wide, y_rows, bias_at + 3, span[0])
+                if h < len(target_halves) - 1:
+                    lse_pass(y_rows, x_cols, running, None, span, (0, rows), h == 0)
+            sent = finish(y_rows, x_cols, span, source_halves, h == 0, *over_tgt)
+        if step == ITERS - 1:
+            break
+        for h, span in enumerate(source_halves):
+            settle(sent[h])
+            lines = lines_of(span)
+            f = FACTOR * (log_a[lines] - joined(row_buf.at[step], n_tgt, lines))
+            set_bias(f, x_wide, x_rows, bias_at, span[0])
+            if h < len(source_halves) - 1:
+                lse_pass(x_rows, y_cols, running, None, span, (0, columns), h == 0)
+        sent = finish(x_rows, y_cols, span, target_halves, h == 0, *over_src)
 
     piece = columns // n_src
     width = math.gcd(piece, WIDTH)
     halves = width // LANES
     parts = []
 
-    def fill(unit):
+    def start_of(unit):
         k, c = divmod(unit, piece // width)
-        start = lax.rem(src + k + 1, n_src) * piece + c * width
-        start = pl.multiple_of(start, width)
-        right = y_cols[:, pl.ds(start, width)]
-        return start, fill_tile(x_rows, right, tile.at[unit % 2])
+        return pl.multiple_of(lax.rem(src + k + 1, n_src) * piece + c * width, width)
+
+    def fill(unit, span, peak):
+        right = y_cols[:, pl.ds(start_of(unit), width)]
+        return fill_tile(x_rows, right, tile.at[unit % 2], span, peak)
 
     units = n_src * (piece // width)
-    ready = fill(0)
+    empty = jnp.full((8, width), -jnp.inf, jnp.float32)
+    ready = empty
+    for h, span in enumerate(source_halves):
+        settle(sent[h])
+        lines = lines_of(span)
+        f = FACTOR * (log_a[lines] - joined(row_buf.at[ITERS - 1], n_tgt, lines))
+        f_ref[lines, :] = UNIT * f
+        set_bias(f, x_wide, x_rows, bias_at, span[0])
+        ready = fill(0, span, ready)
     for unit in range(units):
-        start, peak = ready
+        start, peak = start_of(unit), jnp.max(ready, axis=0, keepdims=True)
         if unit + 1 < units:
-            ready = fill(unit + 1)
+            ready = fill(unit + 1, (0, rows), empty)
         carried = carry_tile(tile.at[unit % 2], peak, scores_t, weights.at[unit % 2])
         for h in range(halves):
             lanes = slice(h * LANES, (h + 1) * LANES)
@@ -230,7 +280,7 @@
             )
             copy.start()
             parts.append(copy)
-    copies = exchange(stat, "src", src, n_src, stat_send, stat_recv)
+    copies = exchange(stat, "src", src, n_src, stat_send, stat_recv, slice(0, 2))
     for copy in copies:
         copy.wait()
     peak = functools.reduce(jnp.maximum, [stat[d, 1] for d in range(n_src)])
@@ -300,14 +350,15 @@
                 pltpu.VMEM((programs + 16, rows), bf16),
                 pltpu.VMEM((2, rows, width), bf16),
                 pltpu.VMEM((columns, programs), f32),
+                pltpu.VMEM((2, max(rows, columns) // LANES, 8, LANES), f32),
                 pltpu.VMEM((ITERS, n_tgt) + dense_r, f32),
                 pltpu.VMEM((ITERS, n_src) + dense_c, f32),
                 pltpu.VMEM((n_src, 2) + dense_c, f32),
                 pltpu.VMEM((n_src, piece, programs), f32),
-                sem((ITERS, n_tgt)),
-                sem((ITERS, n_tgt)),
-                sem((ITERS, n_src)),
-                sem((ITERS, n_src)),
+                sem((ITERS, 2, n_tgt)),
+                sem((ITERS, 2, n_tgt)),
+                sem((ITERS, 2, n_src)),
+                sem((ITERS, 2, n_src)),
                 sem((n_src,)),
                 sem((n_src,)),
                 sem((n_src,)),

time: 63.2 us -> 62.2 us (0.984)
  Pallas kernels: 58 us -> 57 us
    pallas_call x1, Pallas kernels: 58 us -> 57 us  [shards(): pl.pallas_call(functools.partial(kernel, n_src, n_tgt), out_shape=(jax.Sh...]
where the time goes in v2:
time: 62.2 us; the launch traced here: 61.9 us
  Pallas kernels  57 us (92%)
  local copies, waits for them, and re-layouts  4.25 us (7%)
  between operations  0.65 us (1%)
    pallas_call x1, Pallas kernels, shards(): pl.pallas_call(functools.partial(kernel, n_src, n_tgt), out_shape=(jax.Sh...  57 us
    unnamed x7, local copies, waits for them, and re-layouts  4.25 us

profile of v2, /device:TPU:0, one launch (start us, length us, event | category | flops | bytes accessed | tf_op | source)
XLA Modules:
  0.0 61.9 jit_solution(15758585205008109097)
XLA Ops:
  0.6 57.0 %coupling.1 = (f32[16,128]{1,0:T(8,128)}, f32[16,128]{1,0:T(8,128)}, f32[2048,128]{1,0:T(8,128)}) custom-call(bf16[30,2048]{1,0:T(8,128)(2,1)} %xs_ref.1, bf16[30,2048]{1,0:T(8,128)(2,1)} %yt_ref.1, f32[16,128]{1,0:T(8,128)} %bitcast.3, bf16[2048,128]{1,0:T(8,128)(2,1)} %scores_ref.1), custom_call_target="tpu_custom_call" | custom-call | tf_op jit(solution)/shard_map/coupling/pallas_call | solution.py:333
  57.7 0.0 copy-start.1
  57.7 0.7 %copy-done.1 = f32[16,128]{1,0:T(8,128)S(1)} copy-done((f32[16,128]{1,0:T(8,128)S(1)}, f32[16,128]{1,0:T(8,128)}, u32[]{:S(2)}) %copy-start.1) | copy-done | bytes 8216
  58.4 0.0 copy-start
  58.4 0.6 copy.10
  59.0 0.1 copy-done
  59.1 0.6 copy.11
  59.7 2.3 %copy.12 = f32[2048,128]{1,0:T(8,128)} copy(f32[2048,128]{1,0:T(8,128)} %get-tuple-element.14) | data formatting | bytes 2097152
Async XLA Ops:
  57.7 0.7 %copy-start.1 = (f32[16,128]{1,0:T(8,128)S(1)}, f32[16,128]{1,0:T(8,128)}, u32[]{:S(2)}) copy-start(f32[16,128]{1,0:T(8,128)} %get-tuple-element.6) | copy-start | bytes 24580
  58.4 0.7 %copy-start = (f32[16,128]{1,0:T(8,128)S(1)}, f32[16,128]{1,0:T(8,128)}, u32[]{:S(2)}) copy-start(f32[16,128]{1,0:T(8,128)} %get-tuple-element.7) | copy-start | bytes 24580

commit v3 on v2

--- a/solution.py
+++ b/solution.py
@@ -30,10 +30,10 @@
     return base, -(-(3 * base + 16) // LANES) * LANES
 
 
-def augment(coords_ref, wide_ref, columns_ref, scale, source):
-    pcs, cells = coords_ref.shape
+def augment(coords, wide_ref, scale, source):
+    pcs, cells = coords.shape
     base, depth = depth_of(pcs)
-    wide = coords_ref[...].astype(jnp.float32)
+    wide = coords.astype(jnp.float32)
     norm = -0.5 * scale * jnp.sum(wide * wide, axis=0, keepdims=True)
     at = lax.broadcasted_iota(jnp.int32, (16, cells), 0) - (0 if source else 3)
     high, mid, low = split3(norm)
@@ -44,7 +44,6 @@
     for k, piece in enumerate(split3(scale * wide) if source else (wide,) * 3):
         wide_ref[k * base : k * base + pcs, :] = piece
     wide_ref[3 * base : 3 * base + 16, :] = jnp.where(ones, 1.0, extra)
-    columns_ref[...] = wide_ref[...].astype(jnp.bfloat16)
 
 
 def turn(wide_ref, rows_ref, first, last):
@@ -115,7 +114,7 @@
                 lse_ref[pl.ds(tile, 1), :] = top + jnp.log2(total)
         return unused
 
-    lax.fori_loop(0, (end - begin) // width, over_columns, 0)
+    lax.fori_loop(0, (end - begin) // width, over_columns, 0, unroll=True)
 
 
 def fill_tile(rows_ref, right, tile_ref, row_span, peak):
@@ -141,9 +140,9 @@
 
 def kernel(
     n_src, n_tgt, xs_ref, yt_ref, growth_ref, scores_ref, f_ref, g_ref, out_ref,
-    tile, x_wide, y_wide, x_rows, x_cols, y_rows, y_cols, scores_t, weights, partial, running,
-    row_buf, col_buf, stat, received, row_send, row_recv, col_send, col_recv,
-    stat_send, stat_recv, part_send, part_recv, out_send, out_recv,
+    tile, x_wide, y_wide, x_rows, x_cols, y_rows, y_cols, scores_t, weights, running, sums, peaks, pay,
+    row_buf, col_buf, f_all, row_send, row_recv, col_send, col_recv,
+    bulk_send, bulk_recv, pass_send, pass_recv, f_send, f_recv,
 ):
     src, tgt = lax.axis_index("src"), lax.axis_index("tgt")
     barrier = pltpu.get_barrier_semaphore()
@@ -161,9 +160,80 @@
     programs = scores_ref.shape[1]
     scale = 2.0 * LOG2E / (pcs * EPSILON)
     bias_at = 3 * depth_of(pcs)[0] + 8
-    augment(yt_ref, y_wide, y_cols, scale, False)
+    augment(yt_ref[...], y_wide, scale, False)
+    y_cols[...] = y_wide[...].astype(jnp.bfloat16)
     turn(y_wide, y_rows, 0, columns)
-    augment(xs_ref, x_wide, x_cols, scale, True)
+    augment(xs_ref[...], x_wide.at[0], scale, True)
+    x_cols[...] = x_wide[0].astype(jnp.bfloat16)
+
+    pay[0, programs:, :] = jnp.zeros((pay.shape[1] - programs, rows), jnp.float32)
+    pay[0, programs : programs + pcs, :] = xs_ref[...].astype(jnp.float32)
+    for k in range(rows // LANES):
+        cut = slice(k * LANES, (k + 1) * LANES)
+        pay[0, 0:programs, cut] = scores_ref[cut, :].astype(jnp.float32).T
+    scores_t[0, 0:programs, :] = pay[0, 0:programs, :].astype(jnp.bfloat16)
+    for p in range(2):
+        scores_t[p, programs:, :] = jnp.ones((16, rows), jnp.bfloat16)
+
+    bits = [1 << b for b in range(n_src.bit_length() - 1)]
+    core, share = lax.rem(tgt, 2), pay.shape[1] // 4
+
+    def relative(mask):
+        there = src
+        for bit in bits:
+            if mask & bit:
+                there = there + bit - 2 * bit * lax.rem(lax.div(src, bit), 2)
+        return there
+
+    def lines_at(order):
+        return pl.ds(pl.multiple_of((2 * core + order) * share, 8), share)
+
+    bulk, passed = {}, {}
+
+    def ship(order, bit, mask):
+        lines = lines_at(order)
+        copy = pltpu.make_async_remote_copy(
+            src_ref=pay.at[mask, lines], dst_ref=pay.at[mask ^ bit, lines],
+            send_sem=bulk_send.at[order, mask ^ bit], recv_sem=bulk_recv.at[order, mask ^ bit],
+            device_id={"src": relative(bit)}, device_id_type=MESH,
+        )
+        copy.start()
+        bulk[order, mask ^ bit] = copy
+
+    def hand_over(order, mask):
+        if (order, mask) in passed:
+            return
+        bulk[order, mask].wait_recv()
+        lines = lines_at(order)
+        copy = pltpu.make_async_remote_copy(
+            src_ref=pay.at[mask, lines], dst_ref=pay.at[mask, lines],
+            send_sem=pass_send.at[order, mask], recv_sem=pass_recv.at[order, mask],
+            device_id={"tgt": tgt + 1 - 2 * core}, device_id_type=MESH,
+        )
+        copy.start()
+        passed[order, mask] = copy
+
+    orders = [bits, bits[::-1]]
+
+    def ship_first():
+        for order, bit in enumerate(orders):
+            ship(order, bit[0], 0)
+
+    def ship_own():
+        for order, bit in enumerate(orders):
+            for b in bit[1:]:
+                ship(order, b, 0)
+            hand_over(order, bit[0])
+
+    def ship_rest():
+        for t in range(1, len(bits)):
+            for order, bit in enumerate(orders):
+                held = [0]
+                for b in bit[:t]:
+                    held += [m ^ b for m in held]
+                for mask in held[1:]:
+                    hand_over(order, mask)
+                    ship(order, bit[t], mask)
 
     def exchange(buf, axis, me, n, send, recv, lines):
         copies = [
@@ -190,12 +260,10 @@
     def lines_of(span):
         return slice(span[0] // LANES, span[1] // LANES)
 
-    def finish(rows_ref, columns_ref, row_span, spans, fresh, buf, axis, me, n, send, recv, enter=False):
+    def finish(rows_ref, columns_ref, row_span, spans, fresh, buf, axis, me, n, send, recv):
         sent = []
         for h, span in enumerate(spans):
             lse_pass(rows_ref, columns_ref, running, buf.at[me], row_span, span, fresh)
-            if enter and h == 0:
-                pl.semaphore_wait(barrier, n_src + n_tgt - 2)
             sent.append(exchange(buf, axis, me, n, send.at[h], recv.at[h], lines_of(span)))
         return sent
 
@@ -207,13 +275,9 @@
         over_tgt = (row_buf.at[step], "tgt", tgt, n_tgt, row_send.at[step], row_recv.at[step])
         over_src = (col_buf.at[step], "src", src, n_src, col_send.at[step], col_recv.at[step])
         if step == 0:
-            sent = finish(
-                y_rows, x_cols, (0, columns), source_halves, True, *over_tgt, enter=True
-            )
-            for k in range(rows // LANES):
-                cut = slice(k * LANES, (k + 1) * LANES)
-                scores_t[0:programs, cut] = scores_ref[cut, :].astype(jnp.float32).T.astype(jnp.bfloat16)
-            scores_t[programs:, :] = jnp.ones((16, rows), jnp.bfloat16)
+            pl.semaphore_wait(barrier, n_src + n_tgt - 2)
+            ship_first()
+            sent = finish(y_rows, x_cols, (0, columns), source_halves, True, *over_tgt)
         else:
             for h, span in enumerate(target_halves):
                 settle(sent[h])
@@ -229,92 +293,101 @@
             settle(sent[h])
             lines = lines_of(span)
             f = FACTOR * (log_a[lines] - joined(row_buf.at[step], n_tgt, lines))
-            set_bias(f, x_wide, x_rows, bias_at, span[0])
+            set_bias(f, x_wide.at[0], x_rows.at[0], bias_at, span[0])
             if h < len(source_halves) - 1:
-                lse_pass(x_rows, y_cols, running, None, span, (0, columns), h == 0)
-        sent = finish(x_rows, y_cols, span, target_halves, h == 0, *over_src)
-
-    piece = columns // n_src
-    width = math.gcd(piece, WIDTH)
-    halves = width // LANES
-    parts = []
-
-    def start_of(unit):
-        k, c = divmod(unit, piece // width)
-        return pl.multiple_of(lax.rem(src + k + 1, n_src) * piece + c * width, width)
-
-    def fill(unit, span, peak):
-        right = y_cols[:, pl.ds(start_of(unit), width)]
-        return fill_tile(x_rows, right, tile.at[unit % 2], span, peak)
-
-    units = n_src * (piece // width)
+                lse_pass(x_rows.at[0], y_cols, running, None, span, (0, columns), h == 0)
+        sent = finish(x_rows.at[0], y_cols, span, target_halves, h == 0, *over_src)
+        if step == 0:
+            ship_own()
+
+    width = math.gcd(columns, WIDTH)
+    groups, halves = columns // width, width // LANES
     empty = jnp.full((8, width), -jnp.inf, jnp.float32)
+
+    def lanes_of(c):
+        return pl.ds(pl.multiple_of(c * width, width), width)
+
+    def fill(block, c, slot, span, peak):
+        return fill_tile(x_rows.at[block % 2], y_cols[:, lanes_of(c)], tile.at[slot], span, peak)
+
+    def prepare(block):
+        for order in range(2):
+            hand_over(order, block)
+        for order in range(2):
+            passed[order, block].wait_recv()
+        shared[block].wait_recv()
+        slot = block % 2
+        wide_ref, rows_ref = x_wide.at[slot], x_rows.at[slot]
+        augment(pay[block, programs : programs + pcs, :], wide_ref, scale, True)
+        set_bias(f_all[block], wide_ref, rows_ref, bias_at, 0)
+        scores_t[slot, 0:programs, :] = pay[block, 0:programs, :].astype(jnp.bfloat16)
+
+    def carry(block, c, slot, ready):
+        lanes = lanes_of(c)
+        peak = jnp.max(ready, axis=0, keepdims=True)
+        if block > 0:
+            before = peaks[0:1, lanes]
+            peak = jnp.maximum(peak, before)
+        carried = carry_tile(tile.at[slot], peak, scores_t.at[block % 2], weights.at[slot])
+        if block > 0:
+            carried = carried + sums[:, lanes] * jnp.exp2(before - peak)
+        if block < n_src - 1:
+            sums[:, lanes] = carried
+            peaks[0:1, lanes] = peak
+            return
+        mass = carried[programs : programs + 1, :]
+        g = UNIT * FACTOR * (log_b - (peak + jnp.log2(mass)))
+        carried = carried[0:programs, :] / mass
+        for h in range(halves):
+            cut = slice(h * LANES, (h + 1) * LANES)
+            g_ref[pl.ds(c * halves + h, 1), :] = g[:, cut]
+            at = pl.ds(pl.multiple_of(c * width + h * LANES, LANES), LANES)
+            out_ref[at, :] = carried[:, cut].T
+
     ready = empty
     for h, span in enumerate(source_halves):
         settle(sent[h])
         lines = lines_of(span)
         f = FACTOR * (log_a[lines] - joined(row_buf.at[ITERS - 1], n_tgt, lines))
         f_ref[lines, :] = UNIT * f
-        set_bias(f, x_wide, x_rows, bias_at, span[0])
-        ready = fill(0, span, ready)
-    for unit in range(units):
-        start, peak = start_of(unit), jnp.max(ready, axis=0, keepdims=True)
-        if unit + 1 < units:
-            ready = fill(unit + 1, (0, rows), empty)
-        carried = carry_tile(tile.at[unit % 2], peak, scores_t, weights.at[unit % 2])
-        for h in range(halves):
-            lanes = slice(h * LANES, (h + 1) * LANES)
-            stat[src, 0, pl.ds(start // LANES + h, 1), :] = carried[programs : programs + 1, lanes]
-            stat[src, 1, pl.ds(start // LANES + h, 1), :] = peak[:, lanes]
-            at = pl.ds(pl.multiple_of(start + h * LANES, LANES), LANES)
-            partial[at, :] = carried[0:programs, lanes].T
-        k = (unit + 1) * width // piece
-        owner = lax.rem(src + k, n_src)
-        if (unit + 1) * width % piece:
-            continue
-        if k < n_src:
-            copy = pltpu.make_async_remote_copy(
-                src_ref=partial.at[pl.ds(pl.multiple_of(owner * piece, piece), piece), :],
-                dst_ref=received.at[k], send_sem=part_send.at[k], recv_sem=part_recv.at[k],
-                device_id={"src": owner}, device_id_type=MESH,
-            )
-            copy.start()
-            parts.append(copy)
-    copies = exchange(stat, "src", src, n_src, stat_send, stat_recv, slice(0, 2))
-    for copy in copies:
-        copy.wait()
-    peak = functools.reduce(jnp.maximum, [stat[d, 1] for d in range(n_src)])
-    total = sum(stat[d, 0] * jnp.exp2(stat[d, 1] - peak) for d in range(n_src))
-    g_ref[...] = UNIT * FACTOR * (log_b - (peak + jnp.log2(total)))
-    for d in range(n_src):
-        stat[d, 0] = jnp.exp2(stat[d, 1] - peak) / total
-    for copy in parts:
-        copy.wait()
-    first_row = src * (piece // LANES)
-    for q in range(piece // LANES):
-        mine = pl.ds(pl.multiple_of(src * piece + q * LANES, LANES), LANES)
-        result = None
-        for k in range(n_src):
-            sender = lax.rem(src - k + n_src, n_src)
-            share = jnp.broadcast_to(
-                stat[sender, 0, pl.ds(first_row + q, 1), :], (LANES, LANES)
-            ).T
-            block = partial[mine, :] if k == 0 else received[k, q * LANES : (q + 1) * LANES, :]
-            result = share * block if result is None else result + share * block
-        out_ref[mine, :] = result
-    mine = pl.ds(pl.multiple_of(src * piece, piece), piece)
-    copies = [
-        pltpu.make_async_remote_copy(
-            src_ref=out_ref.at[mine, :], dst_ref=out_ref.at[mine, :],
-            send_sem=out_send.at[k], recv_sem=out_recv.at[k],
-            device_id={"src": lax.rem(src + k, n_src)}, device_id_type=MESH,
-        )
-        for k in range(1, n_src)
-    ]
-    for copy in copies:
-        copy.start()
-    for copy in copies:
-        copy.wait()
+        f_all[0, lines, :] = f
+        if h == len(source_halves) - 1:
+            shared = {}
+            for mask in range(1, n_src):
+                shared[mask] = pltpu.make_async_remote_copy(
+                    src_ref=f_all.at[0], dst_ref=f_all.at[mask],
+                    send_sem=f_send.at[mask], recv_sem=f_recv.at[mask],
+                    device_id={"src": relative(mask)}, device_id_type=MESH,
+                )
+                shared[mask].start()
+            ship_rest()
+        set_bias(f, x_wide.at[0], x_rows.at[0], bias_at, span[0])
+        if n_src <= 4:
+            ready = fill(0, 0, 0, span, ready)
+    if n_src <= 4:
+        units = [(block, c) for block in range(n_src) for c in range(groups)]
+        for u, (block, c) in enumerate(units):
+            now = ready
+            if c == 0 and groups > 1 and block + 1 < n_src:
+                for order in range(2):
+                    hand_over(order, block + 1)
+            if c == groups // 2 and block + 1 < n_src:
+                prepare(block + 1)
+            if u + 1 < len(units):
+                ready = fill(*units[u + 1], (u + 1) % 2, (0, rows), empty)
+            carry(block, c, u % 2, now)
+    else:
+        for block in range(n_src):
+            if block > 0:
+                prepare(block)
+
+            def over_groups(c, unused, block=block):
+                carry(block, c, 0, fill(block, c, 0, (0, rows), empty))
+                return unused
+
+            lax.fori_loop(0, groups, over_groups, 0)
+    for copy in [*bulk.values(), *passed.values(), *shared.values()]:
+        copy.wait_send()
 
 
 def solution(mesh):
@@ -323,9 +396,9 @@
     def shards(pcs_source, pcs_target, growth, scores):
         rows, columns = pcs_source.shape[1], pcs_target.shape[1]
         programs = scores.shape[1]
-        piece = columns // n_src
-        width = math.gcd(piece, WIDTH)
-        depth = depth_of(pcs_source.shape[0])[1]
+        width = math.gcd(columns, WIDTH)
+        pcs = pcs_source.shape[0]
+        depth = depth_of(pcs)[1]
         f32, bf16 = jnp.float32, jnp.bfloat16
         sem = pltpu.SemaphoreType.DMA
         whole = pl.BlockSpec(memory_space=pltpu.VMEM)
@@ -341,28 +414,29 @@
             out_specs=(whole,) * 3,
             scratch_shapes=[
                 pltpu.VMEM((2, rows, width), f32),
-                pltpu.VMEM((depth, rows), f32),
+                pltpu.VMEM((2, depth, rows), f32),
                 pltpu.VMEM((depth, columns), f32),
-                pltpu.VMEM((rows, depth), bf16),
+                pltpu.VMEM((2, rows, depth), bf16),
                 pltpu.VMEM((depth, rows), bf16),
                 pltpu.VMEM((columns, depth), bf16),
                 pltpu.VMEM((depth, columns), bf16),
-                pltpu.VMEM((programs + 16, rows), bf16),
+                pltpu.VMEM((2, programs + 16, rows), bf16),
                 pltpu.VMEM((2, rows, width), bf16),
-                pltpu.VMEM((columns, programs), f32),
                 pltpu.VMEM((2, max(rows, columns) // LANES, 8, LANES), f32),
+                pltpu.VMEM((programs + 16, columns), f32),
+                pltpu.VMEM((8, columns), f32),
+                pltpu.VMEM((n_src, -(-(programs + pcs) // 32) * 32, rows), f32),
                 pltpu.VMEM((ITERS, n_tgt) + dense_r, f32),
                 pltpu.VMEM((ITERS, n_src) + dense_c, f32),
-                pltpu.VMEM((n_src, 2) + dense_c, f32),
-                pltpu.VMEM((n_src, piece, programs), f32),
+                pltpu.VMEM((n_src,) + dense_r, f32),
                 sem((ITERS, 2, n_tgt)),
                 sem((ITERS, 2, n_tgt)),
                 sem((ITERS, 2, n_src)),
                 sem((ITERS, 2, n_src)),
-                sem((n_src,)),
-                sem((n_src,)),
-                sem((n_src,)),
-                sem((n_src,)),
+                sem((2, n_src)),
+                sem((2, n_src)),
+                sem((2, n_src)),
+                sem((2, n_src)),
                 sem((n_src,)),
                 sem((n_src,)),
             ],

time: 62.2 us -> 54.5 us (0.88)
  Pallas kernels: 57 us -> 49.3 us
    pallas_call x1, Pallas kernels: 57 us -> 49.3 us  [shards(): pl.pallas_call(functools.partial(kernel, n_src, n_tgt), out_shape=(jax.Sh...]
where the time goes in v3:
time: 54.5 us; the launch traced here: 54.2 us
  Pallas kernels  49.3 us (90%)
  local copies, waits for them, and re-layouts  4.25 us (8%)
  between operations  0.65 us (1%)
    pallas_call x1, Pallas kernels, shards(): pl.pallas_call(functools.partial(kernel, n_src, n_tgt), out_shape=(jax.Sh...  49.3 us
    unnamed x7, local copies, waits for them, and re-layouts  4.25 us

profile of v3, /device:TPU:0, one launch (start us, length us, event | category | flops | bytes accessed | tf_op | source)
XLA Modules:
  0.0 54.2 jit_solution(15645635005488817061)
XLA Ops:
  0.6 49.3 %coupling.1 = (f32[16,128]{1,0:T(8,128)}, f32[16,128]{1,0:T(8,128)}, f32[2048,128]{1,0:T(8,128)}) custom-call(bf16[30,2048]{1,0:T(8,128)(2,1)} %xs_ref.1, bf16[30,2048]{1,0:T(8,128)(2,1)} %yt_ref.1, f32[16,128]{1,0:T(8,128)} %bitcast.3, bf16[2048,128]{1,0:T(8,128)(2,1)} %scores_ref.1), custom_call_target="tpu_custom_call" | custom-call | tf_op jit(solution)/shard_map/coupling/pallas_call | solution.py:406
  49.9 0.0 copy-start.1
  50.0 0.7 %copy-done.1 = f32[16,128]{1,0:T(8,128)S(1)} copy-done((f32[16,128]{1,0:T(8,128)S(1)}, f32[16,128]{1,0:T(8,128)}, u32[]{:S(2)}) %copy-start.1) | copy-done | bytes 8216
  50.6 0.0 copy-start
  50.6 0.6 %copy.10 = f32[2048]{0:T(1024)} copy(f32[2048]{0:T(1024)S(1)} %bitcast.5) | data formatting | bytes 16384
  51.2 0.1 copy-done
  51.3 0.6 %copy.11 = f32[2048]{0:T(1024)} copy(f32[2048]{0:T(1024)S(1)} %bitcast.4) | data formatting | bytes 16384
  51.9 2.3 %copy.12 = f32[2048,128]{1,0:T(8,128)} copy(f32[2048,128]{1,0:T(8,128)} %get-tuple-element.14) | data formatting | bytes 2097152
Async XLA Ops:
  49.9 0.7 %copy-start.1 = (f32[16,128]{1,0:T(8,128)S(1)}, f32[16,128]{1,0:T(8,128)}, u32[]{:S(2)}) copy-start(f32[16,128]{1,0:T(8,128)} %get-tuple-element.6) | copy-start | bytes 24580
  50.6 0.7 %copy-start = (f32[16,128]{1,0:T(8,128)S(1)}, f32[16,128]{1,0:T(8,128)}, u32[]{:S(2)}) copy-start(f32[16,128]{1,0:T(8,128)} %get-tuple-element.7) | copy-start | bytes 24580

commit v4 on v3

--- a/solution.py
+++ b/solution.py
@@ -141,8 +141,8 @@
 def kernel(
     n_src, n_tgt, xs_ref, yt_ref, growth_ref, scores_ref, f_ref, g_ref, out_ref,
     tile, x_wide, y_wide, x_rows, x_cols, y_rows, y_cols, scores_t, weights, running, sums, peaks, pay,
-    row_buf, col_buf, f_all, row_send, row_recv, col_send, col_recv,
-    bulk_send, bulk_recv, pass_send, pass_recv, f_send, f_recv,
+    row_buf, col_buf, f_all, g_all, row_send, row_recv, col_send, col_recv,
+    bulk_send, bulk_recv, pass_send, pass_recv, f_send, f_recv, out_send, out_recv,
 ):
     src, tgt = lax.axis_index("src"), lax.axis_index("tgt")
     barrier = pltpu.get_barrier_semaphore()
@@ -172,7 +172,7 @@
         cut = slice(k * LANES, (k + 1) * LANES)
         pay[0, 0:programs, cut] = scores_ref[cut, :].astype(jnp.float32).T
     scores_t[0, 0:programs, :] = pay[0, 0:programs, :].astype(jnp.bfloat16)
-    for p in range(2):
+    for p in range(scores_t.shape[0]):
         scores_t[p, programs:, :] = jnp.ones((16, rows), jnp.bfloat16)
 
     bits = [1 << b for b in range(n_src.bit_length() - 1)]
@@ -185,55 +185,62 @@
                 there = there + bit - 2 * bit * lax.rem(lax.div(src, bit), 2)
         return there
 
-    def lines_at(order):
-        return pl.ds(pl.multiple_of((2 * core + order) * share, 8), share)
+    early = share // 3 // 8 * 8
+    spans_of_share = [(0, early), (early, share)] if early else [(0, share)]
+    parts = range(len(spans_of_share))
+
+    def lines_at(order, part):
+        low, high = spans_of_share[part]
+        return pl.ds(pl.multiple_of((2 * core + order) * share + low, 8), high - low)
 
     bulk, passed = {}, {}
 
-    def ship(order, bit, mask):
-        lines = lines_at(order)
+    def ship(order, bit, mask, part):
+        lines, there = lines_at(order, part), mask ^ bit
         copy = pltpu.make_async_remote_copy(
-            src_ref=pay.at[mask, lines], dst_ref=pay.at[mask ^ bit, lines],
-            send_sem=bulk_send.at[order, mask ^ bit], recv_sem=bulk_recv.at[order, mask ^ bit],
+            src_ref=pay.at[mask, lines], dst_ref=pay.at[there, lines],
+            send_sem=bulk_send.at[order, there, part], recv_sem=bulk_recv.at[order, there, part],
             device_id={"src": relative(bit)}, device_id_type=MESH,
         )
         copy.start()
-        bulk[order, mask ^ bit] = copy
-
-    def hand_over(order, mask):
-        if (order, mask) in passed:
-            return
-        bulk[order, mask].wait_recv()
-        lines = lines_at(order)
-        copy = pltpu.make_async_remote_copy(
-            src_ref=pay.at[mask, lines], dst_ref=pay.at[mask, lines],
-            send_sem=pass_send.at[order, mask], recv_sem=pass_recv.at[order, mask],
-            device_id={"tgt": tgt + 1 - 2 * core}, device_id_type=MESH,
-        )
-        copy.start()
-        passed[order, mask] = copy
+        bulk[order, there, part] = copy
+
+    def hand_over(mask, chosen=(0, 1)):
+        for part in parts:
+            for order in chosen:
+                if (order, mask, part) in passed:
+                    continue
+                bulk[order, mask, part].wait_recv()
+                lines = lines_at(order, part)
+                copy = pltpu.make_async_remote_copy(
+                    src_ref=pay.at[mask, lines], dst_ref=pay.at[mask, lines],
+                    send_sem=pass_send.at[order, mask, part],
+                    recv_sem=pass_recv.at[order, mask, part],
+                    device_id={"tgt": tgt + 1 - 2 * core}, device_id_type=MESH,
+                )
+                copy.start()
+                passed[order, mask, part] = copy
 
     orders = [bits, bits[::-1]]
 
-    def ship_first():
+    def ship_own(stages, chosen):
+        for t in stages:
+            for part in chosen:
+                for order, bit in enumerate(orders):
+                    ship(order, bit[t], 0, part)
+
+    def ship_rest():
         for order, bit in enumerate(orders):
-            ship(order, bit[0], 0)
-
-    def ship_own():
-        for order, bit in enumerate(orders):
-            for b in bit[1:]:
-                ship(order, b, 0)
-            hand_over(order, bit[0])
-
-    def ship_rest():
+            hand_over(bit[0], (order,))
         for t in range(1, len(bits)):
             for order, bit in enumerate(orders):
                 held = [0]
                 for b in bit[:t]:
                     held += [m ^ b for m in held]
                 for mask in held[1:]:
-                    hand_over(order, mask)
-                    ship(order, bit[t], mask)
+                    hand_over(mask, (order,))
+                    for part in parts:
+                        ship(order, bit[t], mask, part)
 
     def exchange(buf, axis, me, n, send, recv, lines):
         copies = [
@@ -255,6 +262,7 @@
 
     log_a = jnp.log2(growth_ref[...]) - math.log2(rows * n_src)
     log_b = -math.log2(columns * n_tgt)
+    quarters = n_src == 4
     source_halves, target_halves = halves_of(rows), halves_of(columns)
 
     def lines_of(span):
@@ -276,7 +284,8 @@
         over_src = (col_buf.at[step], "src", src, n_src, col_send.at[step], col_recv.at[step])
         if step == 0:
             pl.semaphore_wait(barrier, n_src + n_tgt - 2)
-            ship_first()
+            ship_own(range(1), parts)
+            ship_own(range(1, len(bits)), parts[:1])
             sent = finish(y_rows, x_cols, (0, columns), source_halves, True, *over_tgt)
         else:
             for h, span in enumerate(target_halves):
@@ -298,53 +307,58 @@
                 lse_pass(x_rows.at[0], y_cols, running, None, span, (0, columns), h == 0)
         sent = finish(x_rows.at[0], y_cols, span, target_halves, h == 0, *over_src)
         if step == 0:
-            ship_own()
-
-    width = math.gcd(columns, WIDTH)
+            ship_own(range(1, len(bits)), parts[1:])
+            if quarters:
+                ship_rest()
+
+    width, slots = tile.shape[2], x_rows.shape[0]
     groups, halves = columns // width, width // LANES
+    piece = columns // n_src
     empty = jnp.full((8, width), -jnp.inf, jnp.float32)
 
-    def lanes_of(c):
-        return pl.ds(pl.multiple_of(c * width, width), width)
-
-    def fill(block, c, slot, span, peak):
-        return fill_tile(x_rows.at[block % 2], y_cols[:, lanes_of(c)], tile.at[slot], span, peak)
-
-    def prepare(block):
+    def fill(block, start, slot, span, peak):
+        right = y_cols[:, pl.ds(pl.multiple_of(start, width), width)]
+        return fill_tile(x_rows.at[block % slots], right, tile.at[slot], span, peak)
+
+    def unpack(block):
+        hand_over(block)
         for order in range(2):
-            hand_over(order, block)
-        for order in range(2):
-            passed[order, block].wait_recv()
+            for part in parts:
+                passed[order, block, part].wait_recv()
+        augment(pay[block, programs : programs + pcs, :], x_wide.at[block % slots], scale, True)
+        scores_t[block % slots, 0:programs, :] = pay[block, 0:programs, :].astype(jnp.bfloat16)
+
+    def admit(block):
         shared[block].wait_recv()
-        slot = block % 2
-        wide_ref, rows_ref = x_wide.at[slot], x_rows.at[slot]
-        augment(pay[block, programs : programs + pcs, :], wide_ref, scale, True)
-        set_bias(f_all[block], wide_ref, rows_ref, bias_at, 0)
-        scores_t[slot, 0:programs, :] = pay[block, 0:programs, :].astype(jnp.bfloat16)
-
-    def carry(block, c, slot, ready):
-        lanes = lanes_of(c)
+        slot = block % slots
+        set_bias(f_all[block], x_wide.at[slot], x_rows.at[slot], bias_at, 0)
+
+    def carry(block, start, place, slot, ready):
         peak = jnp.max(ready, axis=0, keepdims=True)
         if block > 0:
-            before = peaks[0:1, lanes]
+            before = peaks[place, 0:1, :]
             peak = jnp.maximum(peak, before)
-        carried = carry_tile(tile.at[slot], peak, scores_t.at[block % 2], weights.at[slot])
+        carried = carry_tile(tile.at[slot], peak, scores_t.at[block % slots], weights.at[slot])
         if block > 0:
-            carried = carried + sums[:, lanes] * jnp.exp2(before - peak)
+            carried = carried + sums[place] * jnp.exp2(before - peak)
         if block < n_src - 1:
-            sums[:, lanes] = carried
-            peaks[0:1, lanes] = peak
+            sums[place] = carried
+            peaks[place, 0:1, :] = peak
             return
         mass = carried[programs : programs + 1, :]
         g = UNIT * FACTOR * (log_b - (peak + jnp.log2(mass)))
         carried = carried[0:programs, :] / mass
         for h in range(halves):
             cut = slice(h * LANES, (h + 1) * LANES)
-            g_ref[pl.ds(c * halves + h, 1), :] = g[:, cut]
-            at = pl.ds(pl.multiple_of(c * width + h * LANES, LANES), LANES)
-            out_ref[at, :] = carried[:, cut].T
-
-    ready = empty
+            at = start + h * LANES
+            owner = lax.div(at, piece)
+            g_all[owner, pl.ds(lax.div(at - owner * piece, LANES), 1), :] = g[:, cut]
+            out_ref[pl.ds(pl.multiple_of(at, LANES), LANES), :] = carried[:, cut].T
+
+    for block in range(1, n_src):
+        if quarters and block < n_src - 1:
+            hand_over(block)
+    ready, shared = empty, {}
     for h, span in enumerate(source_halves):
         settle(sent[h])
         lines = lines_of(span)
@@ -352,7 +366,6 @@
         f_ref[lines, :] = UNIT * f
         f_all[0, lines, :] = f
         if h == len(source_halves) - 1:
-            shared = {}
             for mask in range(1, n_src):
                 shared[mask] = pltpu.make_async_remote_copy(
                     src_ref=f_all.at[0], dst_ref=f_all.at[mask],
@@ -360,32 +373,61 @@
                     device_id={"src": relative(mask)}, device_id_type=MESH,
                 )
                 shared[mask].start()
-            ship_rest()
+            if not quarters:
+                ship_rest()
         set_bias(f, x_wide.at[0], x_rows.at[0], bias_at, span[0])
-        if n_src <= 4:
-            ready = fill(0, 0, 0, span, ready)
-    if n_src <= 4:
-        units = [(block, c) for block in range(n_src) for c in range(groups)]
-        for u, (block, c) in enumerate(units):
-            now = ready
-            if c == 0 and groups > 1 and block + 1 < n_src:
-                for order in range(2):
-                    hand_over(order, block + 1)
-            if c == groups // 2 and block + 1 < n_src:
-                prepare(block + 1)
-            if u + 1 < len(units):
-                ready = fill(*units[u + 1], (u + 1) % 2, (0, rows), empty)
-            carry(block, c, u % 2, now)
+        if quarters:
+            ready = fill(0, src * piece, 0, span, ready)
+
+    gathered = []
+    if quarters:
+        wide = piece // width
+        mine = [(src * piece + c * width, c) for c in range(wide)]
+        spare = [((3 - src) * piece + c * width, wide + c) for c in range(wide)]
+        order = [(0, spot) for spot in mine + spare]
+        order += [(block, spot) for block in range(1, n_src) for spot in mine]
+        order += [(block, spot) for block in range(1, n_src) for spot in spare]
+        for u, (block, spot) in enumerate(order):
+            now, after = ready, order[u + 1] if u + 1 < len(order) else None
+            fresh = after and after[0] > block and u < 2 * wide + (n_src - 1) * wide - 1
+            if fresh and after[0] == 1:
+                carry(block, *spot, u % 2, now)
+                now = None
+                hand_over(n_src - 1)
+            if fresh:
+                unpack(after[0])
+                admit(after[0])
+            if after:
+                ready = fill(after[0], after[1][0], (u + 1) % 2, (0, rows), empty)
+            if now is not None:
+                carry(block, *spot, u % 2, now)
+            if u == 2 * wide + (n_src - 1) * wide - 1:
+                at = pl.ds(pl.multiple_of(src * piece, piece), piece)
+                for k, bit in enumerate(bits):
+                    for slot, ref in enumerate((out_ref.at[at, :], g_all.at[src])):
+                        copy = pltpu.make_async_remote_copy(
+                            src_ref=ref, dst_ref=ref,
+                            send_sem=out_send.at[slot, k], recv_sem=out_recv.at[slot, k],
+                            device_id={"src": relative(bit)}, device_id_type=MESH,
+                        )
+                        copy.start()
+                        gathered.append(copy)
     else:
         for block in range(n_src):
             if block > 0:
-                prepare(block)
+                unpack(block)
+                admit(block)
 
             def over_groups(c, unused, block=block):
-                carry(block, c, 0, fill(block, c, 0, (0, rows), empty))
+                start = c * width
+                carry(block, start, c, 0, fill(block, start, 0, (0, rows), empty))
                 return unused
 
             lax.fori_loop(0, groups, over_groups, 0)
+    for copy in gathered:
+        copy.wait()
+    for k in range(n_src):
+        g_ref[k * (piece // LANES) : (k + 1) * (piece // LANES), :] = g_all[k, 0 : piece // LANES, :]
     for copy in [*bulk.values(), *passed.values(), *shared.values()]:
         copy.wait_send()
 
@@ -396,7 +438,9 @@
     def shards(pcs_source, pcs_target, growth, scores):
         rows, columns = pcs_source.shape[1], pcs_target.shape[1]
         programs = scores.shape[1]
-        width = math.gcd(columns, WIDTH)
+        width, slots = math.gcd(columns, WIDTH), 2
+        if n_src == 4:
+            width, slots = math.gcd(columns // n_src, WIDTH), n_src
         pcs = pcs_source.shape[0]
         depth = depth_of(pcs)[1]
         f32, bf16 = jnp.float32, jnp.bfloat16
@@ -414,31 +458,34 @@
             out_specs=(whole,) * 3,
             scratch_shapes=[
                 pltpu.VMEM((2, rows, width), f32),
-                pltpu.VMEM((2, depth, rows), f32),
+                pltpu.VMEM((slots, depth, rows), f32),
                 pltpu.VMEM((depth, columns), f32),
-                pltpu.VMEM((2, rows, depth), bf16),
+                pltpu.VMEM((slots, rows, depth), bf16),
                 pltpu.VMEM((depth, rows), bf16),
                 pltpu.VMEM((columns, depth), bf16),
                 pltpu.VMEM((depth, columns), bf16),
-                pltpu.VMEM((2, programs + 16, rows), bf16),
+                pltpu.VMEM((slots, programs + 16, rows), bf16),
                 pltpu.VMEM((2, rows, width), bf16),
                 pltpu.VMEM((2, max(rows, columns) // LANES, 8, LANES), f32),
-                pltpu.VMEM((programs + 16, columns), f32),
-                pltpu.VMEM((8, columns), f32),
+                pltpu.VMEM((columns // width, programs + 16, width), f32),
+                pltpu.VMEM((columns // width, 8, width), f32),
                 pltpu.VMEM((n_src, -(-(programs + pcs) // 32) * 32, rows), f32),
                 pltpu.VMEM((ITERS, n_tgt) + dense_r, f32),
                 pltpu.VMEM((ITERS, n_src) + dense_c, f32),
                 pltpu.VMEM((n_src,) + dense_r, f32),
+                pltpu.VMEM((n_src, -(-columns // n_src // (8 * LANES)) * 8, LANES), f32),
                 sem((ITERS, 2, n_tgt)),
                 sem((ITERS, 2, n_tgt)),
                 sem((ITERS, 2, n_src)),
                 sem((ITERS, 2, n_src)),
-                sem((2, n_src)),
-                sem((2, n_src)),
-                sem((2, n_src)),
-                sem((2, n_src)),
+                sem((2, n_src, 2)),
+                sem((2, n_src, 2)),
+                sem((2, n_src, 2)),
+                sem((2, n_src, 2)),
                 sem((n_src,)),
                 sem((n_src,)),
+                sem((2, 2)),
+                sem((2, 2)),
             ],
             compiler_params=pltpu.CompilerParams(
                 collective_id=0, has_side_effects=True, vmem_limit_bytes=60 * 2**20

time: 54.5 us -> 51.3 us (0.941)
  Pallas kernels: 49.3 us -> 46.2 us
    pallas_call x1, Pallas kernels: 49.3 us -> 46.2 us  [shards(): pl.pallas_call(functools.partial(kernel, n_src, n_tgt), out_shape=(jax.Sh...]
where the time goes in v4:
time: 51.3 us; the launch traced here: 51.1 us
  Pallas kernels  46.2 us (90%)
  local copies, waits for them, and re-layouts  4.25 us (8%)
  between operations  0.65 us (1%)
    pallas_call x1, Pallas kernels, shards(): pl.pallas_call(functools.partial(kernel, n_src, n_tgt), out_shape=(jax.Sh...  46.2 us
    unnamed x7, local copies, waits for them, and re-layouts  4.25 us

profile of v4, /device:TPU:0, one launch (start us, length us, event | category | flops | bytes accessed | tf_op | source)
XLA Modules:
  0.0 51.1 jit_solution(10125012494828313434)
XLA Ops:
  0.6 46.2 %coupling.1 = (f32[16,128]{1,0:T(8,128)}, f32[16,128]{1,0:T(8,128)}, f32[2048,128]{1,0:T(8,128)}) custom-call(bf16[30,2048]{1,0:T(8,128)(2,1)} %xs_ref.1, bf16[30,2048]{1,0:T(8,128)(2,1)} %yt_ref.1, f32[16,128]{1,0:T(8,128)} %bitcast.3, bf16[2048,128]{1,0:T(8,128)(2,1)} %scores_ref.1), custom_call_target="tpu_custom_call" | custom-call | tf_op jit(solution)/shard_map/coupling/pallas_call | solution.py:450
  46.8 0.0 copy-start.1
  46.8 0.7 %copy-done.1 = f32[16,128]{1,0:T(8,128)S(1)} copy-done((f32[16,128]{1,0:T(8,128)S(1)}, f32[16,128]{1,0:T(8,128)}, u32[]{:S(2)}) %copy-start.1) | copy-done | bytes 8216
  47.5 0.0 copy-start
  47.5 0.6 %copy.10 = f32[2048]{0:T(1024)} copy(f32[2048]{0:T(1024)S(1)} %bitcast.5) | data formatting | bytes 16384
  48.1 0.1 copy-done
  48.2 0.6 %copy.11 = f32[2048]{0:T(1024)} copy(f32[2048]{0:T(1024)S(1)} %bitcast.4) | data formatting | bytes 16384
  48.8 2.3 %copy.12 = f32[2048,128]{1,0:T(8,128)} copy(f32[2048,128]{1,0:T(8,128)} %get-tuple-element.14) | data formatting | bytes 2097152
Async XLA Ops:
  46.8 0.7 %copy-start.1 = (f32[16,128]{1,0:T(8,128)S(1)}, f32[16,128]{1,0:T(8,128)}, u32[]{:S(2)}) copy-start(f32[16,128]{1,0:T(8,128)} %get-tuple-element.6) | copy-start | bytes 24580
  47.5 0.7 %copy-start = (f32[16,128]{1,0:T(8,128)S(1)}, f32[16,128]{1,0:T(8,128)}, u32[]{:S(2)}) copy-start(f32[16,128]{1,0:T(8,128)} %get-tuple-element.7) | copy-start | bytes 24580

commit v5 on v4

--- a/solution.py
+++ b/solution.py
@@ -355,9 +355,11 @@
             g_all[owner, pl.ds(lax.div(at - owner * piece, LANES), 1), :] = g[:, cut]
             out_ref[pl.ds(pl.multiple_of(at, LANES), LANES), :] = carried[:, cut].T
 
-    for block in range(1, n_src):
-        if quarters and block < n_src - 1:
+    if quarters:
+        for block in range(1, n_src - 1):
             hand_over(block)
+        for block in range(1, n_src - 1):
+            unpack(block)
     ready, shared = empty, {}
     for h, span in enumerate(source_halves):
         settle(sent[h])
@@ -395,7 +397,8 @@
                 now = None
                 hand_over(n_src - 1)
             if fresh:
-                unpack(after[0])
+                if after[0] == n_src - 1:
+                    unpack(after[0])
                 admit(after[0])
             if after:
                 ready = fill(after[0], after[1][0], (u + 1) % 2, (0, rows), empty)
@@ -432,6 +435,15 @@
         copy.wait_send()
 
 
+def deliver(f_ref, g_ref, out_ref, f_end, g_end, out_end, sems):
+    refs = ((f_ref, f_end), (g_ref, g_end), (out_ref, out_end))
+    copies = [pltpu.make_async_copy(a, b, sems.at[k]) for k, (a, b) in enumerate(refs)]
+    for copy in copies:
+        copy.start()
+    for copy in copies:
+        copy.wait()
+
+
 def solution(mesh):
     n_src, n_tgt = mesh.shape["src"], mesh.shape["tgt"]
 
@@ -447,13 +459,12 @@
         sem = pltpu.SemaphoreType.DMA
         whole = pl.BlockSpec(memory_space=pltpu.VMEM)
         dense_r, dense_c = (rows // LANES, LANES), (columns // LANES, LANES)
-        f, g, out = pl.pallas_call(
+        shapes = (
+            pltpu.VMEM(dense_r, f32), pltpu.VMEM(dense_c, f32), pltpu.VMEM((columns, programs), f32)
+        )
+        results = pl.pallas_call(
             functools.partial(kernel, n_src, n_tgt),
-            out_shape=(
-                jax.ShapeDtypeStruct(dense_r, f32),
-                jax.ShapeDtypeStruct(dense_c, f32),
-                jax.ShapeDtypeStruct((columns, programs), f32),
-            ),
+            out_shape=shapes,
             in_specs=[whole] * 4,
             out_specs=(whole,) * 3,
             scratch_shapes=[
@@ -492,6 +503,14 @@
             ),
             name="coupling",
         )(pcs_source, pcs_target, growth.reshape(dense_r), scores)
+        f, g, out = pl.pallas_call(
+            deliver,
+            out_shape=tuple(jax.ShapeDtypeStruct(shape.shape, f32) for shape in shapes),
+            in_specs=[whole] * 3,
+            out_specs=(pl.BlockSpec(memory_space=pl.ANY),) * 3,
+            scratch_shapes=[sem((3,))],
+            name="deliver",
+        )(*[pltpu.with_memory_space_constraint(result, pltpu.VMEM) for result in results])
         return f.reshape(-1), g.reshape(-1), out
 
     in_specs = (P(None, "src"), P(None, "tgt"), P("src"), P("src", None))

time: 51.3 us -> 47.1 us (0.918)
  local copies, waits for them, and re-layouts: 4.25 us -> 0 us
    unnamed x7 -> x0, local copies, waits for them, and re-layouts: 4.25 us -> none
    pallas_call x1 -> x2, Pallas kernels: 46.2 us -> 46.1 us  [the longest x1 45.1 us: shards(): pl.pallas_call(functools.partial(kernel, n_src, n_tgt), out_shape=shapes,...]
where the time goes in v5:
time: 47.1 us; the launch traced here: 46.9 us
  Pallas kernels  46.1 us (98%)
  between operations  0.8 us (2%)
    pallas_call x1, Pallas kernels, shards(): pl.pallas_call(functools.partial(kernel, n_src, n_tgt), out_shape=shapes,...  45.1 us
    pallas_call x1, Pallas kernels, shards(): pl.pallas_call(deliver, out_shape=tuple((jax.ShapeDtypeStruct(shape.shape...  1.01 us

profile of v5, /device:TPU:0, one launch (start us, length us, event | category | flops | bytes accessed | tf_op | source)
XLA Modules:
  0.0 46.9 jit_solution(4110684423227138010)
XLA Ops:
  0.6 45.1 %coupling.1 = (f32[16,128]{1,0:T(8,128)S(1)}, f32[16,128]{1,0:T(8,128)S(1)}, f32[2048,128]{1,0:T(8,128)S(1)}) custom-call(bf16[30,2048]{1,0:T(8,128)(2,1)} %xs_ref.1, bf16[30,2048]{1,0:T(8,128)(2,1)} %yt_ref.1, f32[16,128]{1,0:T(8,128)} %bitcast.3, bf16[2048,128]{1,0:T(8,128)(2,1)} %scores_ref.1), custom_call_target="tpu_custom_call" | custom-call | tf_op jit(solution)/shard_map/coupling/pallas_call | solution.py:465
  45.8 1.0 %deliver.1 = (f32[16,128]{1,0:T(8,128)}, f32[16,128]{1,0:T(8,128)}, f32[2048,128]{1,0:T(8,128)}) custom-call(f32[16,128]{1,0:T(8,128)S(1)} %get-tuple-element.9.f_ref, f32[16,128]{1,0:T(8,128)S(1)} %get-tuple-element.10.g_ref, f32[2048,128]{1,0:T(8,128)S(1)} %get-tuple-element.11.out_ref), custom_call_target="tpu_custom_call" | custom-call | tf_op jit(solution)/shard_map/deliver/pallas_call | solution.py:506

commit v6 on v5

--- a/solution.py
+++ b/solution.py
@@ -185,8 +185,9 @@
                 there = there + bit - 2 * bit * lax.rem(lax.div(src, bit), 2)
         return there
 
-    early = share // 3 // 8 * 8
-    spans_of_share = [(0, early), (early, share)] if early else [(0, share)]
+    early = max(share // 5 // 8 * 8, 8)
+    marks = [0, early, max(share - early, early), share]
+    spans_of_share = list(zip(marks, marks[1:]))
     parts = range(len(spans_of_share))
 
     def lines_at(order, part):
@@ -205,8 +206,8 @@
         copy.start()
         bulk[order, there, part] = copy
 
-    def hand_over(mask, chosen=(0, 1)):
-        for part in parts:
+    def hand_over(mask, chosen=(0, 1), pieces=parts):
+        for part in pieces:
             for order in chosen:
                 if (order, mask, part) in passed:
                     continue
@@ -229,7 +230,7 @@
                 for order, bit in enumerate(orders):
                     ship(order, bit[t], 0, part)
 
-    def ship_rest():
+    def ship_rest(chosen):
         for order, bit in enumerate(orders):
             hand_over(bit[0], (order,))
         for t in range(1, len(bits)):
@@ -239,7 +240,7 @@
                     held += [m ^ b for m in held]
                 for mask in held[1:]:
                     hand_over(mask, (order,))
-                    for part in parts:
+                    for part in chosen:
                         ship(order, bit[t], mask, part)
 
     def exchange(buf, axis, me, n, send, recv, lines):
@@ -309,7 +310,7 @@
         if step == 0:
             ship_own(range(1, len(bits)), parts[1:])
             if quarters:
-                ship_rest()
+                ship_rest(parts[:-1])
 
     width, slots = tile.shape[2], x_rows.shape[0]
     groups, halves = columns // width, width // LANES
@@ -375,8 +376,7 @@
                     device_id={"src": relative(mask)}, device_id_type=MESH,
                 )
                 shared[mask].start()
-            if not quarters:
-                ship_rest()
+            ship_rest(parts[-1:] if quarters else parts)
         set_bias(f, x_wide.at[0], x_rows.at[0], bias_at, span[0])
         if quarters:
             ready = fill(0, src * piece, 0, span, ready)
@@ -387,16 +387,17 @@
         mine = [(src * piece + c * width, c) for c in range(wide)]
         spare = [((3 - src) * piece + c * width, wide + c) for c in range(wide)]
         order = [(0, spot) for spot in mine + spare]
-        order += [(block, spot) for block in range(1, n_src) for spot in mine]
-        order += [(block, spot) for block in range(1, n_src) for spot in spare]
+        order += [(block, spot) for spot in mine + spare for block in range(1, n_src)]
         for u, (block, spot) in enumerate(order):
             now, after = ready, order[u + 1] if u + 1 < len(order) else None
-            fresh = after and after[0] > block and u < 2 * wide + (n_src - 1) * wide - 1
+            fresh = after and after[0] > block and after[1][1] == 0
             if fresh and after[0] == 1:
                 carry(block, *spot, u % 2, now)
                 now = None
-                hand_over(n_src - 1)
+                hand_over(n_src - 1, pieces=parts[:-1])
             if fresh:
+                if after[0] == n_src - 2:
+                    hand_over(n_src - 1)
                 if after[0] == n_src - 1:
                     unpack(after[0])
                 admit(after[0])
@@ -404,13 +405,15 @@
                 ready = fill(after[0], after[1][0], (u + 1) % 2, (0, rows), empty)
             if now is not None:
                 carry(block, *spot, u % 2, now)
-            if u == 2 * wide + (n_src - 1) * wide - 1:
-                at = pl.ds(pl.multiple_of(src * piece, piece), piece)
+            if block == n_src - 1 and spot[1] < wide:
+                at = pl.ds(pl.multiple_of(spot[0], width), width)
+                refs = [out_ref.at[at, :]] + [g_all.at[src]] * (spot[1] == wide - 1)
                 for k, bit in enumerate(bits):
-                    for slot, ref in enumerate((out_ref.at[at, :], g_all.at[src])):
+                    for slot, ref in enumerate(refs):
+                        where = spot[1] if slot == 0 else wide
                         copy = pltpu.make_async_remote_copy(
                             src_ref=ref, dst_ref=ref,
-                            send_sem=out_send.at[slot, k], recv_sem=out_recv.at[slot, k],
+                            send_sem=out_send.at[where, k], recv_sem=out_recv.at[where, k],
                             device_id={"src": relative(bit)}, device_id_type=MESH,
                         )
                         copy.start()
@@ -452,7 +455,7 @@
         programs = scores.shape[1]
         width, slots = math.gcd(columns, WIDTH), 2
         if n_src == 4:
-            width, slots = math.gcd(columns // n_src, WIDTH), n_src
+            width, slots = math.gcd(columns // n_src, WIDTH // 2), n_src
         pcs = pcs_source.shape[0]
         depth = depth_of(pcs)[1]
         f32, bf16 = jnp.float32, jnp.bfloat16
@@ -489,14 +492,14 @@
                 sem((ITERS, 2, n_tgt)),
                 sem((ITERS, 2, n_src)),
                 sem((ITERS, 2, n_src)),
-                sem((2, n_src, 2)),
-                sem((2, n_src, 2)),
-                sem((2, n_src, 2)),
-                sem((2, n_src, 2)),
+                sem((2, n_src, 3)),
+                sem((2, n_src, 3)),
+                sem((2, n_src, 3)),
+                sem((2, n_src, 3)),
                 sem((n_src,)),
                 sem((n_src,)),
-                sem((2, 2)),
-                sem((2, 2)),
+                sem((columns // width + 1, 2)),
+                sem((columns // width + 1, 2)),
             ],
             compiler_params=pltpu.CompilerParams(
                 collective_id=0, has_side_effects=True, vmem_limit_bytes=60 * 2**20

time: 47.1 us -> 45.9 us (0.975)
  Pallas kernels: 46.1 us -> 44.9 us
    pallas_call x1, Pallas kernels: 45.1 us -> 43.9 us  [shards(): pl.pallas_call(functools.partial(kernel, n_src, n_tgt), out_shape=shapes,...]
where the time goes in v6:
time: 45.9 us; the launch traced here: 45.7 us
  Pallas kernels  44.9 us (98%)
  between operations  0.8 us (2%)
    pallas_call x1, Pallas kernels, shards(): pl.pallas_call(functools.partial(kernel, n_src, n_tgt), out_shape=shapes,...  43.9 us
    pallas_call x1, Pallas kernels, shards(): pl.pallas_call(deliver, out_shape=tuple((jax.ShapeDtypeStruct(shape.shape...  1.01 us

profile of v6, /device:TPU:0, one launch (start us, length us, event | category | flops | bytes accessed | tf_op | source)
XLA Modules:
  0.0 45.7 jit_solution(6123416811914945818)
XLA Ops:
  0.6 43.9 %coupling.1 = (f32[16,128]{1,0:T(8,128)S(1)}, f32[16,128]{1,0:T(8,128)S(1)}, f32[2048,128]{1,0:T(8,128)S(1)}) custom-call(bf16[30,2048]{1,0:T(8,128)(2,1)} %xs_ref.1, bf16[30,2048]{1,0:T(8,128)(2,1)} %yt_ref.1, f32[16,128]{1,0:T(8,128)} %bitcast.3, bf16[2048,128]{1,0:T(8,128)(2,1)} %scores_ref.1), custom_call_target="tpu_custom_call" | custom-call | tf_op jit(solution)/shard_map/coupling/pallas_call | solution.py:468
  44.6 1.0 %deliver.1 = (f32[16,128]{1,0:T(8,128)}, f32[16,128]{1,0:T(8,128)}, f32[2048,128]{1,0:T(8,128)}) custom-call(f32[16,128]{1,0:T(8,128)S(1)} %get-tuple-element.9.f_ref, f32[16,128]{1,0:T(8,128)S(1)} %get-tuple-element.10.g_ref, f32[2048,128]{1,0:T(8,128)S(1)} %get-tuple-element.11.out_ref), custom_call_target="tpu_custom_call" | custom-call | tf_op jit(solution)/shard_map/deliver/pallas_call | solution.py:509

commit v7 on v6

--- a/solution.py
+++ b/solution.py
@@ -16,7 +16,7 @@
 LOG2E = math.log2(math.e)
 UNIT = EPSILON / LOG2E
 MESH = pl.DeviceIdType.MESH
-WIDTH, STEP, SUB = 512, 256, 64
+WIDTH, STEP, SUB = 512, 512, 64
 
 
 def split3(value):
@@ -139,11 +139,13 @@
 
 
 def kernel(
-    n_src, n_tgt, xs_ref, yt_ref, growth_ref, scores_ref, f_ref, g_ref, out_ref,
-    tile, x_wide, y_wide, x_rows, x_cols, y_rows, y_cols, scores_t, weights, running, sums, peaks, pay,
+    n_src, n_tgt, xs_ref, yt_ref, growth_ref, scores_far, f_ref, g_ref, out_ref,
+    scores_ref, scores_sem, tile, x_wide, y_wide, x_rows, x_cols, y_rows, y_cols, scores_t, weights, running, sums, peaks, pay,
     row_buf, col_buf, f_all, g_all, row_send, row_recv, col_send, col_recv,
     bulk_send, bulk_recv, pass_send, pass_recv, f_send, f_recv, out_send, out_recv,
 ):
+    fetch = pltpu.make_async_copy(scores_far, scores_ref, scores_sem)
+    fetch.start()
     src, tgt = lax.axis_index("src"), lax.axis_index("tgt")
     barrier = pltpu.get_barrier_semaphore()
     for k in range(1, n_src):
@@ -168,6 +170,7 @@
 
     pay[0, programs:, :] = jnp.zeros((pay.shape[1] - programs, rows), jnp.float32)
     pay[0, programs : programs + pcs, :] = xs_ref[...].astype(jnp.float32)
+    fetch.wait()
     for k in range(rows // LANES):
         cut = slice(k * LANES, (k + 1) * LANES)
         pay[0, 0:programs, cut] = scores_ref[cut, :].astype(jnp.float32).T
@@ -468,9 +471,11 @@
         results = pl.pallas_call(
             functools.partial(kernel, n_src, n_tgt),
             out_shape=shapes,
-            in_specs=[whole] * 4,
+            in_specs=[whole] * 3 + [pl.BlockSpec(memory_space=pl.ANY)],
             out_specs=(whole,) * 3,
             scratch_shapes=[
+                pltpu.VMEM((rows, programs), bf16),
+                sem(()),
                 pltpu.VMEM((2, rows, width), f32),
                 pltpu.VMEM((slots, depth, rows), f32),
                 pltpu.VMEM((depth, columns), f32),

time: 45.9 us -> 45.7 us (level)
  no operation moved by 1% of the time
where the time goes in v7:
time: 45.7 us; the launch traced here: 45.5 us
  Pallas kernels  44.7 us (98%)
  between operations  0.8 us (2%)
    pallas_call x1, Pallas kernels, shards(): pl.pallas_call(functools.partial(kernel, n_src, n_tgt), out_shape=shapes,...  43.7 us
    pallas_call x1, Pallas kernels, shards(): pl.pallas_call(deliver, out_shape=tuple((jax.ShapeDtypeStruct(shape.shape...  1.01 us

profile of v7, /device:TPU:0, one launch (start us, length us, event | category | flops | bytes accessed | tf_op | source)
XLA Modules:
  0.0 45.5 jit_solution(14930721157102960021)
XLA Ops:
  0.6 43.7 %coupling.1 = (f32[16,128]{1,0:T(8,128)S(1)}, f32[16,128]{1,0:T(8,128)S(1)}, f32[2048,128]{1,0:T(8,128)S(1)}) custom-call(bf16[30,2048]{1,0:T(8,128)(2,1)} %xs_ref.1, bf16[30,2048]{1,0:T(8,128)(2,1)} %yt_ref.1, f32[16,128]{1,0:T(8,128)} %bitcast.3, bf16[2048,128]{1,0:T(8,128)(2,1)} %scores_far.1), custom_call_target="tpu_custom_call" | custom-call | tf_op jit(solution)/shard_map/coupling/pallas_call | solution.py:471
  44.3 1.0 %deliver.1 = (f32[16,128]{1,0:T(8,128)}, f32[16,128]{1,0:T(8,128)}, f32[2048,128]{1,0:T(8,128)}) custom-call(f32[16,128]{1,0:T(8,128)S(1)} %get-tuple-element.9.f_ref, f32[16,128]{1,0:T(8,128)S(1)} %get-tuple-element.10.g_ref, f32[2048,128]{1,0:T(8,128)S(1)} %get-tuple-element.11.out_ref), custom_call_target="tpu_custom_call" | custom-call | tf_op jit(solution)/shard_map/deliver/pallas_call | solution.py:514

commit v8 on v7

--- a/solution.py
+++ b/solution.py
@@ -181,12 +181,15 @@
     bits = [1 << b for b in range(n_src.bit_length() - 1)]
     core, share = lax.rem(tgt, 2), pay.shape[1] // 4
 
+    def across(me, mask):
+        there = me
+        for b in range(mask.bit_length()):
+            if mask >> b & 1:
+                there = there + (1 << b) - (2 << b) * lax.rem(lax.div(me, 1 << b), 2)
+        return there
+
     def relative(mask):
-        there = src
-        for bit in bits:
-            if mask & bit:
-                there = there + bit - 2 * bit * lax.rem(lax.div(src, bit), 2)
-        return there
+        return across(src, mask)
 
     early = max(share // 5 // 8 * 8, 8)
     marks = [0, early, max(share - early, early), share]
@@ -251,9 +254,9 @@
             pltpu.make_async_remote_copy(
                 src_ref=buf.at[me, lines], dst_ref=buf.at[me, lines],
                 send_sem=send.at[k], recv_sem=recv.at[k],
-                device_id={axis: lax.rem(me + k, n)}, device_id_type=MESH,
+                device_id={axis: across(me, k)}, device_id_type=MESH,
             )
-            for k in range(1, n)
+            for k in range(n - 1, 0, -1)
         ]
         for copy in copies:
             copy.start()

time: 45.7 us -> 45.7 us (level)
  no operation moved by 1% of the time
where the time goes in v8:
time: 45.7 us; the launch traced here: 45.5 us
  Pallas kernels  44.7 us (98%)
  between operations  0.8 us (2%)
    pallas_call x1, Pallas kernels, shards(): pl.pallas_call(functools.partial(kernel, n_src, n_tgt), out_shape=shapes,...  43.7 us
    pallas_call x1, Pallas kernels, shards(): pl.pallas_call(deliver, out_shape=tuple((jax.ShapeDtypeStruct(shape.shape...  1.01 us

profile of v8, /device:TPU:0, one launch (start us, length us, event | category | flops | bytes accessed | tf_op | source)
XLA Modules:
  0.0 45.5 jit_solution(961427028287046809)
XLA Ops:
  0.6 43.7 %coupling.1 = (f32[16,128]{1,0:T(8,128)S(1)}, f32[16,128]{1,0:T(8,128)S(1)}, f32[2048,128]{1,0:T(8,128)S(1)}) custom-call(bf16[30,2048]{1,0:T(8,128)(2,1)} %xs_ref.1, bf16[30,2048]{1,0:T(8,128)(2,1)} %yt_ref.1, f32[16,128]{1,0:T(8,128)} %bitcast.3, bf16[2048,128]{1,0:T(8,128)(2,1)} %scores_far.1), custom_call_target="tpu_custom_call" | custom-call | tf_op jit(solution)/shard_map/coupling/pallas_call | solution.py:474
  44.3 1.0 %deliver.1 = (f32[16,128]{1,0:T(8,128)}, f32[16,128]{1,0:T(8,128)}, f32[2048,128]{1,0:T(8,128)}) custom-call(f32[16,128]{1,0:T(8,128)S(1)} %get-tuple-element.9.f_ref, f32[16,128]{1,0:T(8,128)S(1)} %get-tuple-element.10.g_ref, f32[2048,128]{1,0:T(8,128)S(1)} %get-tuple-element.11.out_ref), custom_call_target="tpu_custom_call" | custom-call | tf_op jit(solution)/shard_map/deliver/pallas_call | solution.py:517
